TPU v7x, 128 devices: a whole 4x4x4 slice. The times are simulated.
128 devices in a mesh: tok: 8 (over y, x_lo), tp: 16 (over z, x_hi, core).
Axes of the slice: x: 4 (x_hi: 2, x_lo: 2; x = x_hi * 2 + x_lo), y: 4, z: 4, core: 2. Of those that a mesh axis runs over, the one named last changes fastest.
Arguments:
- source: bfloat16 [2048, 8192], P('tp', 'tok'), may hold values from -6 to 6
- row_token: int32 [2048], replicated, may hold values from 0 to 2047, each once
- seg_ids: int32 [8, 256], P('tok'), may hold values from 0 to 3, never falling along the last dimension, each value on 1 to 128 neighbouring positions
- stitch_weight: bfloat16 [8192, 8192], P('tok', 'tp'), may hold values from -0.0625 to 0.0625
- norm_gain: float32 [8192], replicated, may hold values from 0.5 to 1.5
- q_weight: bfloat16 [8192, 8192], P(None, 'tp'), may hold values from -2 to 2
- kv_weight: bfloat16 [8192, 2048], P(None, 'tp'), may hold values from -2 to 2
- o_weight: bfloat16 [8192, 8192], P('tp'), may hold values from -0.0625 to 0.0625
- out_grad: bfloat16 [2048, 8192], P('tok', 'tp'), may hold values from -6 to 6
Outputs:
- layer_out: bfloat16 [2048, 8192], P('tok', 'tp')
- stitch_grad: float32 [8192, 8192], P('tok', 'tp')
Inputs may be any that keep to these rules, and one draw needn't show every extreme that they name: `row_token`: each token index appears exactly once. `seg_ids`: within a pack the ids never fall; a document holds 1 to 128 tokens.
All inputs are finite; a program needn't handle non-finite values.
Results may differ from a plain program's by a relative error of at most 0.024.
Values may be sent and summed in bfloat16 or wider, within the bound.
A program may use at most 128 MiB of HBM per device.

v0:
```python
import math

import jax
import jax.numpy as jnp
from jax import lax
from jax.sharding import PartitionSpec as P

HD = 128


epsilon = 1e-05


def swapped(value, axis, distance):
    mask = 2**distance
    pairs = [(source, source ^ mask) for source in range(lax.axis_size(axis))]
    return lax.ppermute(value, axis, pairs)


def frequencies():
    exponent = jnp.arange(0, HD, 2).astype(jnp.float32) / HD
    plain_rate = 500000.0 ** (-exponent)
    wavelength = 2.0 * math.pi / plain_rate
    smoothing = (8192.0 / wavelength - 1.0) / 3.0
    blended = (1.0 - smoothing) * plain_rate / 8.0 + smoothing * plain_rate
    return jnp.where(
        wavelength < 2048.0, plain_rate, jnp.where(wavelength > 8192.0, plain_rate / 8.0, blended)
    )


def rotate(vector_in, cosine_table, sine_table):
    half_size = vector_in.shape[-1] // 2
    first_half = vector_in[..., :half_size]
    second = vector_in[..., half_size:]
    return jnp.concatenate(
        [
            first_half * cosine_table - second * sine_table,
            second * cosine_table + first_half * sine_table,
        ],
        axis=-1,
    )


def unrotate(vector_in, cosine_table, sine_table):
    half_size = vector_in.shape[-1] // 2
    first_half = vector_in[..., :half_size]
    second = vector_in[..., half_size:]
    return jnp.concatenate(
        [
            first_half * cosine_table + second * sine_table,
            second * cosine_table - first_half * sine_table,
        ],
        axis=-1,
    )


def body(
    source, row_token, seg_ids, stitch_weight, norm_gain, q_weight, kv_weight, o_weight, out_grad
):
    tp_rank = lax.axis_index("tp")
    pack_len = seg_ids.shape[1]
    score_scale = 1.0 / math.sqrt(HD)
    gathered = lax.all_gather(source, "tp", axis=0, tiled=True)
    every_row_stack = gathered.shape[0]
    placing = (
        jnp.zeros((every_row_stack,), jnp.int32)
        .at[row_token]
        .set(jnp.arange(every_row_stack, dtype=jnp.int32))
    )
    column_block = jnp.take(gathered, placing, axis=0)
    token_rows = lax.all_to_all(column_block, "tok", split_axis=0, concat_axis=1, tiled=True)
    features = token_rows
    hidden_cols = jnp.dot(
        features,
        lax.all_gather(stitch_weight, "tok", axis=0, tiled=True),
        preferred_element_type=jnp.float32,
    )
    hidden_bf = hidden_cols.astype(jnp.bfloat16)
    hidden_all = lax.all_gather(hidden_bf, "tp", axis=1, tiled=True)
    hidden_f = hidden_all.astype(jnp.float32)
    inv_rms = lax.rsqrt(jnp.mean(hidden_f * hidden_f, axis=1, keepdims=True) + epsilon)
    normed = (hidden_f * inv_rms * norm_gain).astype(jnp.bfloat16)
    seg_row = seg_ids[0]
    earlier = jnp.sum((seg_row[None, :] < seg_row[:, None]).astype(jnp.int32), axis=1)
    index_row = jnp.arange(pack_len, dtype=jnp.int32)
    angles = (index_row - earlier).astype(jnp.float32)[:, None] * frequencies()[None, :]
    cosines = jnp.cos(angles)[:, None, :]
    sine_table = jnp.sin(angles)[:, None, :]
    allowed = (
        (seg_row[:, None] == seg_row[None, :]) & (index_row[None, :] <= index_row[:, None])
    ).astype(jnp.int32)
    local_heads = q_weight.shape[1] // HD
    kv_local = 1
    repeat = local_heads // kv_local
    queries = rotate(
        jnp.dot(normed, q_weight, preferred_element_type=jnp.float32).reshape(
            pack_len, local_heads, HD
        ),
        cosines,
        sine_table,
    ).astype(jnp.bfloat16)
    projected = jnp.dot(normed, kv_weight, preferred_element_type=jnp.float32)
    is_key = tp_rank % 2 == 0
    own_part = jnp.where(
        is_key, rotate(projected, cosines[:, 0], sine_table[:, 0]), projected
    ).astype(jnp.bfloat16)
    partner = swapped(own_part, "tp", 0)
    per_head_keys = jnp.where(is_key, own_part, partner)[:, None, :]
    per_head_values = jnp.where(is_key, partner, own_part)[:, None, :]
    per_head_queries = queries.reshape(pack_len, kv_local, repeat, HD)
    scores = (
        jnp.einsum(
            "nkej,wkj->kenw", per_head_queries, per_head_keys, preferred_element_type=jnp.float32
        )
        * score_scale
    )
    scores = jnp.where(allowed != 0, scores, -1e30)
    row_max = jnp.max(scores, axis=-1, keepdims=True)
    exponents = jnp.exp(scores - row_max)
    attention = exponents / jnp.sum(exponents, axis=-1, keepdims=True)
    attention_half_precision = attention.astype(jnp.bfloat16)
    context = jnp.einsum(
        "cnfo,och->fcnh",
        attention_half_precision,
        per_head_values,
        preferred_element_type=jnp.float32,
    ).astype(jnp.bfloat16)
    context = context.reshape(pack_len, local_heads * HD)
    attended = lax.psum_scatter(
        jnp.dot(context, o_weight, preferred_element_type=jnp.float32).astype(jnp.bfloat16),
        "tp",
        scatter_dimension=1,
        tiled=True,
    ).astype(jnp.float32)
    layer_out = (hidden_bf.astype(jnp.float32) + attended).astype(jnp.bfloat16)
    gradient_every_row = lax.all_gather(out_grad, "tp", axis=1, tiled=True)
    grad_context = jnp.dot(
        gradient_every_row, o_weight.T, preferred_element_type=jnp.float32
    ).astype(jnp.bfloat16)
    context_gradient = grad_context.reshape(pack_len, kv_local, repeat, HD)
    grad_probs = jnp.einsum(
        "nkej,wkj->kenw", context_gradient, per_head_values, preferred_element_type=jnp.float32
    )
    centered = grad_probs - jnp.sum(grad_probs * attention, axis=-1, keepdims=True)
    score_gradient = (attention * centered * score_scale).astype(jnp.bfloat16)
    query_grad = jnp.einsum(
        "cnfo,och->fcnh", score_gradient, per_head_keys, preferred_element_type=jnp.float32
    )
    grad_queries = unrotate(
        query_grad.reshape(pack_len, local_heads, HD), cosines, sine_table
    ).astype(jnp.bfloat16)
    key_part = jnp.einsum(
        "bwlf,lbwj->fbj", score_gradient, per_head_queries, preferred_element_type=jnp.float32
    )
    value_part = jnp.einsum(
        "bwlf,lbwj->fbj",
        attention_half_precision,
        context_gradient,
        preferred_element_type=jnp.float32,
    )
    outgoing = jnp.where(is_key, value_part, key_part)[:, 0]
    incoming = swapped(outgoing.astype(jnp.bfloat16), "tp", 0).astype(outgoing.dtype)
    own_sum = jnp.where(is_key, key_part, value_part)[:, 0] + incoming
    grad_pairs = jnp.where(
        is_key, unrotate(own_sum, cosines[:, 0], sine_table[:, 0]), own_sum
    ).astype(jnp.bfloat16)
    grad_normed = jnp.dot(
        grad_queries.reshape(pack_len, local_heads * HD),
        q_weight.T,
        preferred_element_type=jnp.float32,
    )
    grad_normed = grad_normed + jnp.dot(grad_pairs, kv_weight.T, preferred_element_type=jnp.float32)
    weighted = norm_gain * grad_normed
    cubed = inv_rms * inv_rms * inv_rms
    norm_term = inv_rms * weighted - hidden_f * cubed * jnp.mean(
        weighted * hidden_f, axis=1, keepdims=True
    )
    grad_sum = lax.psum_scatter(
        norm_term.astype(jnp.bfloat16), "tp", scatter_dimension=1, tiled=True
    ).astype(jnp.float32)
    grad_hidden = (out_grad.astype(jnp.float32) + grad_sum).astype(jnp.bfloat16)
    features = token_rows
    stitch_grad = lax.psum_scatter(
        lax.dot_general(
            features, grad_hidden, (((0,), (0,)), ((), ())), preferred_element_type=jnp.float32
        ).astype(jnp.bfloat16),
        "tok",
        scatter_dimension=0,
        tiled=True,
    ).astype(jnp.float32)
    return (layer_out, stitch_grad)


def solution(mesh):
    placed = (
        P("tp", "tok"),
        P(),
        P("tok", None),
        P("tok", "tp"),
        P(),
        P(None, "tp"),
        P(None, "tp"),
        P("tp", None),
        P("tok", "tp"),
    )
    return jax.shard_map(
        body,
        mesh=mesh,
        in_specs=placed,
        out_specs=(P("tok", "tp"), P("tok", "tp")),
        check_vma=False,
    )
```

profile of v0, /device:TPU:0, one launch (start us, length us, event | category | flops | bytes accessed | tf_op | source)
XLA Modules:
  0.0 782.9 jit_solution(5317935610867189701)
XLA Ops:
  10.1 8.0 %scatter_custom_fusion = s32[2048]{0:T(1024)S(1)} fusion(s32[2048]{0:T(1024)S(1)} %compare_select_fusion.1, s32[2048]{0:T(1024)S(1)} %iota.19, s32[]{:T(128)} %constant.22.clone.1), kind=kCustom, calls=%fused_computation.84 | custom fusion | bytes 8196 | tf_op jit(solution)/shard_map/scatter | solution.py:68
  18.2 50.2 %all-gather.5.cloned.1.call-done = bf16[2048,1024]{1,0:T(8,128)(2,1)} async-done(((bf16[128,1024]{1,0:T(8,128)(2,1)}), bf16[2048,1024]{1,0:T(8,128)(2,1)}) %all-gather.5.cloned.1.call-update) | async-done | bytes 4194320 | tf_op jit(solution)/shard_map/all_gather | solution.py:63
  68.4 13.6 %gather_fusion = bf16[2048,1024]{1,0:T(8,128)(2,1)} fusion(bf16[2048,1024]{1,0:T(8,128)(2,1)} %all-gather.5.cloned.1.call-done, s32[2048]{0:T(1024)S(1)} %fusion.43), kind=kCustom, calls=%fused_computation | custom fusion | bytes 8396800 | tf_op jit(solution)/shard_map/jit(_take)/gather | solution.py:70
  82.1 6.4 copy.25
  88.5 2.6 broadcast_select_fusion
  91.1 99.6 %all_to_all.16 = bf16[8,256,1024]{1,2,0:T(8,128)(2,1)} all-to-all(bf16[8,256,1024]{1,2,0:T(8,128)(2,1)S(1)} %broadcast_select_fusion), channel_id=1, replica_groups=mesh['tok'=8,'tp'=16] {'tok'}, dimensions={0} | all-to-all | bytes 8388608 | tf_op jit(solution)/shard_map/all_to_all | solution.py:71
  190.7 90.4 %all-gather.7.cloned.1.call-done = bf16[8192,512]{1,0:T(8,128)(2,1)} async-done(((bf16[1024,512]{1,0:T(8,128)(2,1)}), bf16[8192,512]{1,0:T(8,128)(2,1)}) %all-gather.7.cloned.1.call-update) | async-done | bytes 8388624 | tf_op jit(solution)/shard_map/all_gather | solution.py:75
  281.1 7.7 convolution_convert_fusion.4
  289.6 0.7 convert_compare_fusion
  290.3 51.0 %all-gather.11.cloned.1.call-done = bf16[256,8192]{1,0:T(8,128)(2,1)} async-done(((bf16[256,512]{1,0:T(8,128)(2,1)}), bf16[256,8192]{1,0:T(8,128)(2,1)}) %all-gather.11.cloned.1.call-update) | async-done | bytes 4194320 | tf_op jit(solution)/shard_map/all_gather | solution.py:136
  341.4 7.0 convolution_convert_fusion.3
  348.4 0.8 copy.53
  349.2 49.5 %all-gather.9.cloned.1.call-done = bf16[256,8192]{1,0:T(8,128)(2,1)} async-done(((bf16[256,512]{1,0:T(8,128)(2,1)}), bf16[256,8192]{1,0:T(8,128)(2,1)}) %all-gather.9.cloned.1.call-update) | async-done | bytes 4194320 | tf_op jit(solution)/shard_map/all_gather | solution.py:79
  398.7 3.3 fusion.1
  402.5 3.9 fusion.12
  407.3 5.8 fusion.10
  413.9 1.3 fusion.52
  415.4 1.9 convolution_bitcast_fusion.2
  418.4 1.2 convolution_bitcast_fusion.1
  419.8 0.9 pad_maximum_fusion.1
  420.7 1.1 copy.36
  421.8 0.9 fusion.36
  422.8 5.9 fusion.53
  429.2 5.3 fusion.7
  434.5 5.9 fusion.6
  441.1 7.7 convolution_convert_fusion.1
  448.9 70.1 %reduce-scatter.6.cloned.1.call-done = bf16[256,512]{1,0:T(8,128)(2,1)} async-done(((bf16[256,8192]{1,0:T(8,128)(2,1)}), bf16[256,512]{1,0:T(8,128)(2,1)}) %reduce-scatter.6.cloned.1.call-update) | async-done | bytes 262160 | tf_op jit(solution)/shard_map/reduce_scatter | solution.py:178
  519.0 7.8 %convolution_convert_fusion = bf16[8192,512]{1,0:T(8,128)(2,1)} fusion(bf16[256,8192]{0,1:T(8,128)(2,1)} %bitcast.85, bf16[256,512]{1,0:T(8,128)(2,1)} %reduce-scatter.6.cloned.1.call-done, bf16[256,512]{1,0:T(8,128)(2,1)S(1)} %copy-done.4), kind=kOutput, calls=%fused_computation.6 | convolution fusion | flops 2152202240 | bytes 13107200 | tf_op jit(solution)/shard_map/dot_general | solution.py:184
  526.8 76.0 %reduce-scatter.4.cloned.1.call-done = bf16[256,512]{1,0:T(8,128)(2,1)} async-done(((bf16[256,8192]{1,0:T(8,128)(2,1)}), bf16[256,512]{1,0:T(8,128)(2,1)}) %reduce-scatter.4.cloned.1.call-update) | async-done | bytes 262160 | tf_op jit(solution)/shard_map/reduce_scatter | solution.py:129
  602.9 1.7 add_convert_fusion.2
  604.6 168.6 %reduce-scatter.8.cloned.1.call-done = bf16[1024,512]{1,0:T(8,128)(2,1)} async-done(((bf16[8192,512]{1,0:T(8,128)(2,1)}), bf16[1024,512]{1,0:T(8,128)(2,1)}) %reduce-scatter.8.cloned.1.call-update) | async-done | bytes 1048592 | tf_op jit(solution)/shard_map/reduce_scatter | solution.py:183
  773.2 2.8 convert_element_type.137
  (78 shorter events, 8.4 us)
Async XLA Ops:
  7.2 395.4 %copy-start = (bf16[8192,128]{1,0:T(8,128)(2,1)S(1)}, bf16[8192,128]{1,0:T(8,128)(2,1)}, u32[]{:S(2)}) copy-start(bf16[8192,128]{1,0:T(8,128)(2,1)} %param.15) | copy-start | bytes 6291460
  7.2 61.2 %all-gather.5.cloned.1.call-start = ((), (), s32[]{:S(2)}) async-start(), calls=%async_computation.4 | async-start | bytes 4456448 | tf_op jit(solution)/shard_map/all_gather | solution.py:63
  7.9 273.2 %all-gather.7.cloned.1.call-start = ((), (), s32[]{:S(2)}) async-start(), calls=%async_computation.5 | async-start | bytes 9437184 | tf_op jit(solution)/shard_map/all_gather | solution.py:75
  8.7 332.7 %all-gather.11.cloned.1.call-start = ((), (), s32[]{:S(2)}) async-start(), calls=%async_computation.8 | async-start | bytes 4456448 | tf_op jit(solution)/shard_map/all_gather | solution.py:136
  9.4 389.3 %all-gather.9.cloned.1.call-start = ((), (), s32[]{:S(2)}) async-start(), calls=%async_computation.6 | async-start | bytes 4456448 | tf_op jit(solution)/shard_map/all_gather | solution.py:79
  281.1 7.8 copy-start.13
  288.9 230.1 %reduce-scatter.6.cloned.1.call-start = ((), (), s32[]{:S(2)}) async-start(), calls=%async_computation.9 | async-start | bytes 4456448 | tf_op jit(solution)/shard_map/reduce_scatter | solution.py:178
  290.3 112.2 %copy-start.11 = (f32[8192]{0:T(1024)S(1)}, f32[8192]{0:T(1024)}, u32[]{:S(2)}) copy-start(f32[8192]{0:T(1024)} %param.13) | copy-start | bytes 98308
  398.7 8.6 %copy-start.1 = (bf16[256,8192]{1,0:T(8,128)(2,1)S(1)}, bf16[256,8192]{1,0:T(8,128)(2,1)}, u32[]{:S(2)}) copy-start(bf16[256,8192]{1,0:T(8,128)(2,1)} %all-gather.9.cloned.1.call-done) | copy-start | bytes 12582916
  402.5 10.7 %copy-start.15 = (f32[256]{0:T(256)}, f32[256]{0:T(256)S(1)}, u32[]{:S(2)}) copy-start(f32[256]{0:T(256)S(1)} %get-tuple-element.15) | copy-start | bytes 3076
  406.8 10.5 %copy-start.5 = (bf16[256,128]{0,1:T(8,128)(2,1)}, bf16[256,128]{0,1:T(8,128)(2,1)S(1)}, u32[]{:S(2)}) copy-start(bf16[256,128]{0,1:T(8,128)(2,1)S(1)} %fusion.22) | copy-start | bytes 196612
  406.8 7.1 collective-permute-start
  413.4 3.9 copy-start.8
  413.9 3.8 copy-start.9
  422.7 6.1 collective-permute-start.1
  422.8 6.0 copy-start.7
  422.8 6.3 copy-start.2
  422.8 6.3 copy-start.12
  429.2 5.3 copy-start.14
  429.2 5.3 copy-start.16
  434.5 6.2 copy-start.6
  434.5 6.2 copy-start.10
  440.4 162.4 %reduce-scatter.4.cloned.1.call-start = ((), (), s32[]{:S(2)}) async-start(), calls=%async_computation.7 | async-start | bytes 4456448 | tf_op jit(solution)/shard_map/reduce_scatter | solution.py:129
  441.1 77.9 %copy-start.4 = (bf16[256,512]{1,0:T(8,128)(2,1)S(1)}, bf16[256,512]{1,0:T(8,128)(2,1)}, u32[]{:S(2)}) copy-start(bf16[256,512]{1,0:T(8,128)(2,1)} %param.17) | copy-start | bytes 786436
  448.8 154.0 %copy-start.3 = (bf16[256,512]{1,0:T(8,128)(2,1)S(1)}, bf16[256,512]{1,0:T(8,128)(2,1)}, u32[]{:S(2)}) copy-start(bf16[256,512]{1,0:T(8,128)(2,1)} %convolution_convert_fusion.4) | copy-start | bytes 786436
  448.8 324.4 %reduce-scatter.8.cloned.1.call-start = ((), (), s32[]{:S(2)}) async-start(), calls=%async_computation.10 | async-start | bytes 9437184 | tf_op jit(solution)/shard_map/reduce_scatter | solution.py:183
Sparse Core Ops, SparseCore 0:
  10.5 57.8 all-gather.4
  70.1 211.0 all-gather.6
  283.5 57.8 all-gather.10
  344.2 54.5 all-gather.8
  440.5 78.4 reduce-scatter.5
  523.4 79.4 reduce-scatter.3
  605.3 167.9 reduce-scatter.7
where the time goes:
time: 784 us; the launch traced here: 783 us
  waiting for transfers between devices  558 us (71%)
  blocking collectives  99.6 us (13%)
  matrix products  56.8 us (7%)
  local copies, waits for them, and re-layouts  30.9 us (4%)
  other arithmetic  22 us (3%)
  between operations  14.5 us (2%)
    reduce_scatter x1, waiting for transfers between devices, body(): lax.psum_scatter(lax.dot_general(features, grad_hidden, (((0,), (0,)), ((...  169 us
    all_to_all x1, blocking collectives, body(): lax.all_to_all(column_block, 'tok', split_axis=0, concat_axis=1, tiled=True)  99.6 us
    all_gather x1, waiting for transfers between devices, body(): lax.all_gather(stitch_weight, 'tok', axis=0, tiled=True)  90.4 us
    reduce_scatter x1, waiting for transfers between devices, body(): lax.psum_scatter(jnp.dot(context, o_weight, preferred_element_type=jnp.fl...  76 us
    reduce_scatter x1, waiting for transfers between devices, body(): lax.psum_scatter(norm_term.astype(jnp.bfloat16), 'tp', scatter_dimension=...  70.1 us
    all_gather x1, waiting for transfers between devices, body(): gradient_every_row = lax.all_gather(out_grad, 'tp', axis=1, tiled=True)  51 us
    all_gather x1, waiting for transfers between devices, body(): gathered = lax.all_gather(source, 'tp', axis=0, tiled=True)  50.2 us
    all_gather x1, waiting for transfers between devices, body(): hidden_all = lax.all_gather(hidden_bf, 'tp', axis=1, tiled=True)  49.5 us
  transfers between devices with their start and end apart: 9, of which 7 were waited for; matrix products, arithmetic and copies ran while one was open for 10% of the time, Pallas kernels for 0%

commit v1 on v0

--- a/solution.py
+++ b/solution.py
@@ -67,15 +67,11 @@
         .at[row_token]
         .set(jnp.arange(every_row_stack, dtype=jnp.int32))
     )
-    column_block = jnp.take(gathered, placing, axis=0)
-    token_rows = lax.all_to_all(column_block, "tok", split_axis=0, concat_axis=1, tiled=True)
-    features = token_rows
-    hidden_cols = jnp.dot(
-        features,
-        lax.all_gather(stitch_weight, "tok", axis=0, tiled=True),
-        preferred_element_type=jnp.float32,
-    )
-    hidden_bf = hidden_cols.astype(jnp.bfloat16)
+    token_rows = jnp.take(gathered, placing, axis=0)
+    hidden_part = jnp.dot(token_rows, stitch_weight, preferred_element_type=jnp.float32)
+    hidden_bf = lax.psum_scatter(
+        hidden_part.astype(jnp.bfloat16), "tok", scatter_dimension=0, tiled=True
+    )
     hidden_all = lax.all_gather(hidden_bf, "tp", axis=1, tiled=True)
     hidden_f = hidden_all.astype(jnp.float32)
     inv_rms = lax.rsqrt(jnp.mean(hidden_f * hidden_f, axis=1, keepdims=True) + epsilon)
@@ -179,15 +175,10 @@
         norm_term.astype(jnp.bfloat16), "tp", scatter_dimension=1, tiled=True
     ).astype(jnp.float32)
     grad_hidden = (out_grad.astype(jnp.float32) + grad_sum).astype(jnp.bfloat16)
-    features = token_rows
-    stitch_grad = lax.psum_scatter(
-        lax.dot_general(
-            features, grad_hidden, (((0,), (0,)), ((), ())), preferred_element_type=jnp.float32
-        ).astype(jnp.bfloat16),
-        "tok",
-        scatter_dimension=0,
-        tiled=True,
-    ).astype(jnp.float32)
+    every_grad = lax.all_gather(grad_hidden, "tok", axis=0, tiled=True)
+    stitch_grad = lax.dot_general(
+        token_rows, every_grad, (((0,), (0,)), ((), ())), preferred_element_type=jnp.float32
+    )
     return (layer_out, stitch_grad)
 
 

time: 784 us -> 523 us (0.67)
  waiting for transfers between devices: 558 us -> 412 us
  blocking collectives: 99.6 us -> 0 us
    reduce_scatter x1, waiting for transfers between devices: 169 us -> 49.6 us  [body(): lax.psum_scatter(hidden_part.astype(jnp.bfloat16), 'tok', scatter_dimensi...]
    all_to_all x1 -> x0, blocking collectives: 99.6 us -> none  [body(): lax.all_to_all(column_block, 'tok', split_axis=0, concat_axis=1, tiled=True)]
    all_gather x1, waiting for transfers between devices: 90.4 us -> 51.5 us  [body(): every_grad = lax.all_gather(grad_hidden, 'tok', axis=0, tiled=True)]
    gather x2 -> x1, local copies, waits for them, and re-layouts: 20.1 us -> 13.7 us  [body(): token_rows = jnp.take(gathered, placing, axis=0)]
  transfers between devices with their start and end apart: 9 -> 9, of which waited for: 7 -> 7; matrix products, arithmetic and copies ran while one was open for 10% -> 8% of each run, Pallas kernels for 0% -> 0%
where the time goes in v1:
time: 523 us; the launch traced here: 521 us
  waiting for transfers between devices  412 us (79%)
  matrix products  50.8 us (10%)
  local copies, waits for them, and re-layouts  25 us (5%)
  other arithmetic  18.3 us (3%)
  between operations  14.5 us (3%)
    reduce_scatter x1, waiting for transfers between devices, body(): lax.psum_scatter(jnp.dot(context, o_weight, preferred_element_type=jnp.fl...  82.1 us
    reduce_scatter x1, waiting for transfers between devices, body(): lax.psum_scatter(norm_term.astype(jnp.bfloat16), 'tp', scatter_dimension=...  69.6 us
    all_gather x1, waiting for transfers between devices, body(): gradient_every_row = lax.all_gather(out_grad, 'tp', axis=1, tiled=True)  57.1 us
    all_gather x1, waiting for transfers between devices, body(): gathered = lax.all_gather(source, 'tp', axis=0, tiled=True)  51.7 us
    all_gather x1, waiting for transfers between devices, body(): every_grad = lax.all_gather(grad_hidden, 'tok', axis=0, tiled=True)  51.5 us
    reduce_scatter x1, waiting for transfers between devices, body(): lax.psum_scatter(hidden_part.astype(jnp.bfloat16), 'tok', scatter_dimensi...  49.6 us
    all_gather x1, waiting for transfers between devices, body(): hidden_all = lax.all_gather(hidden_bf, 'tp', axis=1, tiled=True)  48.9 us
    gather x1, local copies, waits for them, and re-layouts, body(): token_rows = jnp.take(gathered, placing, axis=0)  13.7 us
  transfers between devices with their start and end apart: 9, of which 7 were waited for; matrix products, arithmetic and copies ran while one was open for 8% of the time, Pallas kernels for 0%

profile of v1, /device:TPU:0, one launch (start us, length us, event | category | flops | bytes accessed | tf_op | source)
XLA Modules:
  0.0 521.5 jit_solution(18185422710442002973)
XLA Ops:
  7.2 0.7 all-gather.5.cloned.1.call-update
  8.0 0.7 compare_select_fusion.1
  8.7 8.0 %scatter_custom_fusion = s32[2048]{0:T(1024)S(1)} fusion(s32[2048]{0:T(1024)S(1)} %compare_select_fusion.1, s32[2048]{0:T(1024)S(1)} %iota.19, s32[]{:T(128)} %constant.22.clone.1), kind=kCustom, calls=%fused_computation.84 | custom fusion | bytes 8196 | tf_op jit(solution)/shard_map/scatter | solution.py:68
  16.8 51.7 %all-gather.5.cloned.1.call-done = bf16[2048,1024]{1,0:T(8,128)(2,1)} async-done(((bf16[128,1024]{1,0:T(8,128)(2,1)}), bf16[2048,1024]{1,0:T(8,128)(2,1)}) %all-gather.5.cloned.1.call-update) | async-done | bytes 4194320 | tf_op jit(solution)/shard_map/all_gather | solution.py:63
  68.4 13.7 %gather_fusion = bf16[2048,1024]{1,0:T(8,128)(2,1)} fusion(bf16[2048,1024]{1,0:T(8,128)(2,1)} %all-gather.5.cloned.1.call-done, s32[2048]{0:T(1024)S(1)} %fusion.44), kind=kCustom, calls=%fused_computation | custom fusion | bytes 8396800 | tf_op jit(solution)/shard_map/jit(_take)/gather | solution.py:70
  82.1 6.0 %convolution_convert_fusion.1 = bf16[2048,512]{1,0:T(8,128)(2,1)} fusion(bf16[1024,512]{1,0:T(8,128)(2,1)S(1)} %copy-done.19, bf16[2048,1024]{1,0:T(8,128)(2,1)} %gather_fusion, pred[2048]{0:T(1024)(128)(4,1)S(1)} %compare_and_fusion), kind=kOutput, calls=%fused_computation.17 | convolution fusion | flops 2150629376 | bytes 7342080 | tf_op jit(solution)/shard_map/dot_general | solution.py:71
  88.2 0.7 all-gather.9.cloned.1.call-update
  88.9 49.6 %reduce-scatter.4.cloned.1.call-done = bf16[256,512]{1,0:T(8,128)(2,1)} async-done(((bf16[2048,512]{1,0:T(8,128)(2,1)}), bf16[256,512]{1,0:T(8,128)(2,1)}) %reduce-scatter.4.cloned.1.call-update) | async-done | bytes 262160 | tf_op jit(solution)/shard_map/reduce_scatter | solution.py:72
  139.3 0.7 convert_compare_fusion
  140.0 57.1 %all-gather.9.cloned.1.call-done = bf16[256,8192]{1,0:T(8,128)(2,1)} async-done(((bf16[256,512]{1,0:T(8,128)(2,1)}), bf16[256,8192]{1,0:T(8,128)(2,1)}) %all-gather.9.cloned.1.call-update) | async-done | bytes 4194320 | tf_op jit(solution)/shard_map/all_gather | solution.py:132
  197.0 7.0 %convolution_convert_fusion.3 = bf16[256,512]{1,0:T(8,128)(2,1)S(1)} fusion(bf16[256,8192]{1,0:T(8,128)(2,1)} %all-gather.9.cloned.1.call-done, bf16[512,8192]{1,0:T(8,128)(2,1)} %param.16), kind=kOutput, calls=%fused_computation.25 | convolution fusion | flops 2147614720 | bytes 12845056 | tf_op jit(solution)/shard_map/dot_general | solution.py:133
  204.1 0.8 copy.52
  204.9 48.9 %all-gather.7.cloned.1.call-done = bf16[256,8192]{1,0:T(8,128)(2,1)} async-done(((bf16[256,512]{1,0:T(8,128)(2,1)}), bf16[256,8192]{1,0:T(8,128)(2,1)}) %all-gather.7.cloned.1.call-update) | async-done | bytes 4194320 | tf_op jit(solution)/shard_map/all_gather | solution.py:75
  253.8 3.3 fusion.1
  257.7 1.7 fusion.13
  260.3 5.8 %fusion.11 = f32[256,512]{1,0:T(8,128)S(1)} fusion(bf16[8192,512]{1,0:T(8,128)(2,1)} %param.14, bf16[256,8192]{1,0:T(8,128)(2,1)S(1)} %copy-done.1, f32[8192]{0:T(1024)S(1)} %copy-done.11, f32[256]{0:T(256)S(1)} %get-tuple-element.15), kind=kOutput, calls=%fused_computation.26 | convolution fusion | flops 2155872256 | bytes 13140992 | tf_op jit(solution)/shard_map/dot_general | solution.py:92
  266.8 1.3 fusion.55
  268.3 1.0 convolution_bitcast_fusion.2
  270.4 1.2 convolution_bitcast_fusion.1
  271.8 0.9 pad_maximum_fusion.1
  272.7 1.1 copy.35
  273.8 0.9 fusion.37
  274.9 5.9 %fusion.56 = f32[256,8192]{1,0:T(8,128)S(1)} fusion(bf16[256,512]{0,1:T(8,128)(2,1)S(1)} %bitcast.79, bf16[8192,512]{1,0:T(8,128)(2,1)} %param.14), kind=kOutput, calls=%fused_computation.99 | convolution fusion | flops 2147483648 | bytes 17039360 | tf_op jit(solution)/shard_map/dot_general | solution.py:163
  281.2 5.3 %fusion.7 = (f32[256]{0:T(256)S(1)}, f32[256,8192]{1,0:T(8,128)}) fusion(bf16[256,8192]{1,0:T(8,128)(2,1)S(1)} %copy-done.2, f32[256,8192]{1,0:T(8,128)S(1)} %fusion.56, bf16[8192,128]{1,0:T(8,128)(2,1)S(1)} %copy-done, f32[256,128]{0,1:T(8,128)S(1)} %bitcast_add_fusion, bf16[256,64]{0,1:T(8,128)(2,1)S(1)} %get-tuple-element.9, ...), kind=kOutput, calls=%fused_computation.15 | convolution fusion | flops 547520256 | bytes 23299072 | tf_op jit(solution)/shard_map/dot_general | solution.py:168
  286.5 5.8 %fusion.6 = bf16[256,8192]{1,0:T(8,128)(2,1)} fusion(bf16[256,8192]{1,0:T(8,128)(2,1)S(1)} %copy-done.2, f32[256,8192]{1,0:T(8,128)} %get-tuple-element.21, f32[256]{0:T(256)S(1)} %broadcast_multiply_fusion, f32[256]{0:T(256)S(1)} %copy-done.14, f32[256]{0:T(256)S(1)} %copy-done.16), kind=kLoop, calls=%fused_computation.14 | loop fusion | flops 12582912 | bytes 16780288 | tf_op jit(solution)/shard_map/convert_element_type | solution.py:175
  293.6 7.7 %convolution_convert_fusion = bf16[256,8192]{1,0:T(8,128)(2,1)} fusion(bf16[256,512]{0,1:T(8,128)(2,1)S(1)} %bitcast.80, bf16[512,8192]{1,0:T(8,128)(2,1)} %param.16), kind=kOutput, calls=%fused_computation.8 | convolution fusion | flops 2149580800 | bytes 12845056 | tf_op jit(solution)/shard_map/dot_general | solution.py:126
  301.4 69.6 %reduce-scatter.8.cloned.1.call-done = bf16[256,512]{1,0:T(8,128)(2,1)} async-done(((bf16[256,8192]{1,0:T(8,128)(2,1)}), bf16[256,512]{1,0:T(8,128)(2,1)}) %reduce-scatter.8.cloned.1.call-update) | async-done | bytes 262160 | tf_op jit(solution)/shard_map/reduce_scatter | solution.py:174
  370.9 1.7 add_convert_fusion
  372.7 82.1 %reduce-scatter.6.cloned.1.call-done = bf16[256,512]{1,0:T(8,128)(2,1)} async-done(((bf16[256,8192]{1,0:T(8,128)(2,1)}), bf16[256,512]{1,0:T(8,128)(2,1)}) %reduce-scatter.6.cloned.1.call-update) | async-done | bytes 262160 | tf_op jit(solution)/shard_map/reduce_scatter | solution.py:125
  454.8 1.7 add_convert_fusion.2
  456.5 51.5 %all-gather.11.cloned.1.call-done = bf16[2048,512]{1,0:T(8,128)(2,1)} async-done(((bf16[256,512]{1,0:T(8,128)(2,1)}), bf16[2048,512]{1,0:T(8,128)(2,1)}) %all-gather.11.cloned.1.call-update) | async-done | bytes 2097168 | tf_op jit(solution)/shard_map/all_gather | solution.py:178
  508.0 6.6 %fusion.8 = f32[1024,512]{1,0:T(8,128)} fusion(bf16[2048,512]{1,0:T(8,128)(2,1)} %all-gather.11.cloned.1.call-done, bf16[2048,1024]{1,0:T(8,128)(2,1)} %gather_fusion, pred[2048]{0:T(1024)(128)(4,1)S(1)} %copy-done.18), kind=kOutput, calls=%fused_computation.18 | convolution fusion | flops 2149580800 | bytes 8390656 | tf_op jit(solution)/shard_map/dot_general | solution.py:179
  (80 shorter events, 6.3 us)
Async XLA Ops:
  7.2 250.5 %copy-start = (bf16[8192,128]{1,0:T(8,128)(2,1)S(1)}, bf16[8192,128]{1,0:T(8,128)(2,1)}, u32[]{:S(2)}) copy-start(bf16[8192,128]{1,0:T(8,128)(2,1)} %param.15) | copy-start | bytes 6291460
  7.2 61.2 %all-gather.5.cloned.1.call-start = ((), (), s32[]{:S(2)}) async-start(), calls=%async_computation.3 | async-start | bytes 4456448 | tf_op jit(solution)/shard_map/all_gather | solution.py:63
  7.9 130.6 %reduce-scatter.4.cloned.1.call-start = ((), (), s32[]{:S(2)}) async-start(), calls=%async_computation.4 | async-start | bytes 2359296 | tf_op jit(solution)/shard_map/reduce_scatter | solution.py:72
  16.7 65.4 %copy-start.17 = (pred[2048]{0:T(1024)(128)(4,1)}, pred[2048]{0:T(1024)(128)(4,1)S(1)}, u32[]{:S(2)}) copy-start(pred[2048]{0:T(1024)(128)(4,1)S(1)} %compare_and_fusion) | copy-start | bytes 6148
  16.8 65.4 %copy-start.19 = (bf16[1024,512]{1,0:T(8,128)(2,1)S(1)}, bf16[1024,512]{1,0:T(8,128)(2,1)}, u32[]{:S(2)}) copy-start(bf16[1024,512]{1,0:T(8,128)(2,1)} %param.12) | copy-start | bytes 3145732
  82.1 56.5 %copy-start.13 = (s32[1,256]{1,0:T(1,128)S(1)}, s32[1,256]{1,0:T(1,128)}, u32[]{:S(2)}) copy-start(s32[1,256]{1,0:T(1,128)} %param.11) | copy-start | bytes 3076
  88.1 108.9 %all-gather.9.cloned.1.call-start = ((), (), s32[]{:S(2)}) async-start(), calls=%async_computation.7 | async-start | bytes 4456448 | tf_op jit(solution)/shard_map/all_gather | solution.py:132
  88.9 164.9 %all-gather.7.cloned.1.call-start = ((), (), s32[]{:S(2)}) async-start(), calls=%async_computation.5 | async-start | bytes 4456448 | tf_op jit(solution)/shard_map/all_gather | solution.py:75
  138.5 232.4 %reduce-scatter.8.cloned.1.call-start = ((), (), s32[]{:S(2)}) async-start(), calls=%async_computation.8 | async-start | bytes 4456448 | tf_op jit(solution)/shard_map/reduce_scatter | solution.py:174
  204.1 53.6 %copy-start.11 = (f32[8192]{0:T(1024)S(1)}, f32[8192]{0:T(1024)}, u32[]{:S(2)}) copy-start(f32[8192]{0:T(1024)} %param.13) | copy-start | bytes 98308
  253.8 3.9 copy-start.1
  257.6 2.6 copy-start.15
  259.8 9.6 %copy-start.5 = (bf16[256,128]{0,1:T(8,128)(2,1)}, bf16[256,128]{0,1:T(8,128)(2,1)S(1)}, u32[]{:S(2)}) copy-start(bf16[256,128]{0,1:T(8,128)(2,1)S(1)} %fusion.23) | copy-start | bytes 196612
  259.8 7.1 %collective-permute-start = (bf16[256,128]{0,1:T(8,128)(2,1)S(1)}, bf16[256,128]{0,1:T(8,128)(2,1)S(1)}, u32[]{:S(2)}, u32[]{:S(2)}) collective-permute-start(bf16[256,128]{0,1:T(8,128)(2,1)S(1)} %fusion.23), channel_id=1, source_target_pairs={{0,1},{1,0},{2,3},{3,2},{4,5},{5,4},{6,7},{7,6},{8,9},{9,8},{10,11... | collective-permute-start | bytes 196616 | tf_op jit(solution)/shard_map/ppermute | solution.py:17
  266.3 2.0 copy-start.8
  266.8 2.8 copy-start.9
  274.7 6.1 %collective-permute-start.1 = (bf16[256,128]{0,1:T(8,128)(2,1)S(1)}, bf16[256,128]{0,1:T(8,128)(2,1)S(1)}, u32[]{:S(2)}, u32[]{:S(2)}) collective-permute-start(bf16[256,128]{0,1:T(8,128)(2,1)S(1)} %fusion.37), channel_id=1, source_target_pairs={{0,1},{1,0},{2,3},{3,2},{4,5},{5,4},{6,7},{7,6},{8,9},{9,8},{10,11... | collective-permute-start | bytes 196616 | tf_op jit(solution)/shard_map/ppermute | solution.py:17
  274.8 6.0 %copy-start.7 = (f32[128,256]{1,0:T(8,128)S(1)}, f32[128,256]{1,0:T(8,128)}, u32[]{:S(2)}) copy-start(f32[128,256]{1,0:T(8,128)} %convolution_bitcast_fusion.2) | copy-start | bytes 393220
  274.8 6.3 %copy-start.2 = (bf16[256,8192]{1,0:T(8,128)(2,1)S(1)}, bf16[256,8192]{1,0:T(8,128)(2,1)}, u32[]{:S(2)}) copy-start(bf16[256,8192]{1,0:T(8,128)(2,1)} %all-gather.7.cloned.1.call-done) | copy-start | bytes 12582916
  274.8 6.3 %copy-start.12 = (f32[8192]{0:T(1024)S(1)}, f32[8192]{0:T(1024)}, u32[]{:S(2)}) copy-start(f32[8192]{0:T(1024)} %param.13) | copy-start | bytes 98308
  281.2 5.3 %copy-start.14 = (f32[256]{0:T(256)S(1)}, f32[256]{0:T(256)}, u32[]{:S(2)}) copy-start(f32[256]{0:T(256)} %get-tuple-element.14) | copy-start | bytes 3076
  281.2 5.3 %copy-start.16 = (f32[256]{0:T(256)S(1)}, f32[256]{0:T(256)}, u32[]{:S(2)}) copy-start(f32[256]{0:T(256)} %copy-done.15) | copy-start | bytes 3076
  292.4 0.8 copy-start.6
  292.4 0.9 copy-start.10
  292.4 162.4 %reduce-scatter.6.cloned.1.call-start = ((), (), s32[]{:S(2)}) async-start(), calls=%async_computation.6 | async-start | bytes 4456448 | tf_op jit(solution)/shard_map/reduce_scatter | solution.py:125
  301.3 69.7 %copy-start.3 = (bf16[256,512]{1,0:T(8,128)(2,1)S(1)}, bf16[256,512]{1,0:T(8,128)(2,1)}, u32[]{:S(2)}) copy-start(bf16[256,512]{1,0:T(8,128)(2,1)} %param.17) | copy-start | bytes 786436
  301.3 153.5 %copy-start.4 = (bf16[256,512]{1,0:T(8,128)(2,1)S(1)}, bf16[256,512]{1,0:T(8,128)(2,1)}, u32[]{:S(2)}) copy-start(bf16[256,512]{1,0:T(8,128)(2,1)} %reduce-scatter.4.cloned.1.call-done) | copy-start | bytes 786436
  301.3 206.7 %copy-start.18 = (pred[2048]{0:T(1024)(128)(4,1)S(1)}, pred[2048]{0:T(1024)(128)(4,1)}, u32[]{:S(2)}) copy-start(pred[2048]{0:T(1024)(128)(4,1)} %copy-done.17) | copy-start | bytes 6148
  301.3 206.7 %all-gather.11.cloned.1.call-start = ((), (), s32[]{:S(2)}) async-start(), calls=%async_computation.9 | async-start | bytes 2359296 | tf_op jit(solution)/shard_map/all_gather | solution.py:178
Sparse Core Ops, SparseCore 0:
  10.5 57.8 all-gather.4
  88.3 50.1 reduce-scatter.3
  140.8 56.1 all-gather.8
  199.2 54.5 all-gather.6
  292.5 78.3 reduce-scatter.7
  375.3 79.4 reduce-scatter.5
  457.0 50.9 all-gather.10

commit v2 on v1

v2 whole, which is shorter than its diff:
```python
import math

import jax
import jax.numpy as jnp
from jax import lax
from jax.experimental import pallas as pl
from jax.experimental.pallas import tpu as pltpu
from jax.sharding import PartitionSpec as P

HD = 128


epsilon = 1e-05


def frequencies():
    exponent = jnp.arange(0, HD, 2).astype(jnp.float32) / HD
    plain_rate = 500000.0 ** (-exponent)
    wavelength = 2.0 * math.pi / plain_rate
    smoothing = (8192.0 / wavelength - 1.0) / 3.0
    blended = (1.0 - smoothing) * plain_rate / 8.0 + smoothing * plain_rate
    return jnp.where(
        wavelength < 2048.0, plain_rate, jnp.where(wavelength > 8192.0, plain_rate / 8.0, blended)
    )


class Group:
    def __init__(self, axis):
        tok, tp = lax.axis_index("tok"), lax.axis_index("tp")
        self.axis, self.tok, self.tp = axis, tok, tp
        if axis == "tp":
            self.ring, self.pair, self.core = tp // 4, (tp // 2) % 2, tp % 2
        else:
            self.ring, self.pair, self.core = tok // 2, tok % 2, 0

    def index(self, step, across, sibling=0):
        ring = lax.rem(self.ring + step, 4)
        pair = 1 - self.pair if across else self.pair
        if self.axis == "tp":
            core = 1 - self.core if sibling else self.core
            return ring * 4 + pair * 2 + core
        return ring * 2 + pair

    def device(self, step, across, sibling=0):
        index = self.index(step, across, sibling)
        return (self.tok, index) if self.axis == "tp" else (index, self.tp)

    def peers(self):
        found = [self.device(step, 0) for step in (1, 2, 3)] + [self.device(0, 1)]
        return found + ([self.device(0, 0, 1)] if self.axis == "tp" else [])


class Wire:
    def __init__(self, send, recv):
        self.send, self.recv, self.slots, self.sent = send, recv, {}, []

    def slot(self, key):
        return self.recv.at[self.slots.setdefault(key, len(self.slots))]

    def put(self, src, dst, device, key):
        copy = pltpu.make_async_remote_copy(
            src_ref=src,
            dst_ref=dst,
            send_sem=self.send.at[len(self.sent)],
            recv_sem=self.slot(key),
            device_id=device,
            device_id_type=pl.DeviceIdType.MESH,
        )
        copy.start()
        self.sent.append(copy)

    def got(self, view, device, key):
        pltpu.make_async_remote_copy(
            src_ref=view,
            dst_ref=view,
            send_sem=self.send.at[0],
            recv_sem=self.slot(key),
            device_id=device,
            device_id_type=pl.DeviceIdType.MESH,
        ).wait_recv()

    def drain(self):
        for copy in self.sent:
            copy.wait_send()


def greet(*groups):
    barrier = pltpu.get_barrier_semaphore()
    peers = [peer for group in groups for peer in group.peers()]
    for peer in peers:
        pl.semaphore_signal(
            barrier, inc=1, device_id=peer, device_id_type=pl.DeviceIdType.MESH
        )
    pl.semaphore_wait(barrier, len(peers))


def wide(value):
    return value.astype(jnp.float32)


def gather_steps(group, wire, shard, whole, cut, local, name, ready):
    two_cores = group.axis == "tp"

    def pass_on(step, across, half):
        if two_cores:
            view = whole(group.index(step, across), half)
            wire.put(view, view, group.device(0, 0, 1), (name, "core", step, across, half))

    def arrived(step, across, half):
        view = whole(group.index(step, across), half)
        wire.got(view, group.device(0, 1), (name, step, across, half))

    def complete(step, across):
        if two_cores:
            for half in (0, 1):
                view = whole(group.index(step, across, 1), half)
                wire.got(view, group.device(0, 0, 1), (name, "core", step, across, half))
        ready(step, across)

    own = group.index(0, 0)
    wire.put(shard(0), whole(own, 0), group.device(0, 1), (name, 0, 1, 0))
    for half in (1, 0):
        for step in (1, 3, 2):
            wire.put(
                shard(half), whole(own, half), group.device(step, 0), (name, 4 - step, 0, half)
            )
    wire.put(shard(1), whole(own, 1), group.device(0, 1), (name, 0, 1, 1))
    kept = [pltpu.make_async_copy(shard(half), whole(own, half), local.at[half]) for half in (0, 1)]
    for copy in kept:
        copy.start()
    if two_cores:
        for half in (0, 1):
            wire.put(
                shard(half), whole(own, half), group.device(0, 0, 1), (name, "core", 0, 0, half)
            )
    for copy in kept:
        copy.wait()
    complete(0, 0)
    yield
    arrived(0, 1, 0)
    view = whole(group.index(0, 1), 0)
    for step in (1, 3, 2):
        wire.put(view, view, group.device(step, 0), (name, 4 - step, 1, 0))
    pass_on(0, 1, 0)
    for step in (1, 3, 2):
        arrived(step, 0, 1)
        view = whole(group.index(step, 0), 1)
        wire.put(view, view, group.device(0, 1), (name, step, 1, 1))
        pass_on(step, 0, 1)
    yield
    for step in (1, 3, 2):
        arrived(step, 0, 0)
        pass_on(step, 0, 0)
    arrived(0, 1, 1)
    pass_on(0, 1, 1)
    yield
    for step in (1, 3, 2):
        complete(step, 0)
    complete(0, 1)
    yield
    for step in (1, 3, 2):
        for half in (0, 1):
            arrived(step, 1, half)
            pass_on(step, 1, half)
    yield
    for step in (1, 3, 2):
        complete(step, 1)


ORDER = [(step, 1) for step in (0, 1, 3, 2)] + [(step, 0) for step in (1, 3, 2, 0)]


def core_steps(group, wire, term, mine, leaving, by_core, name):
    for step, across in ORDER:
        leaving[step, across] = term(group.index(step, across, 1))
        wire.put(
            leaving.at[step, across],
            by_core.at[step, across],
            group.device(0, 0, 1),
            (name, "core", step, across),
        )
        mine[step, across] = term(group.index(step, across))
        yield
        wire.got(by_core.at[step, across], group.device(0, 0, 1), (name, "core", step, across))
        mine[step, across] = (wide(mine[step, across]) + wide(by_core[step, across])).astype(
            jnp.bfloat16
        )
        yield step, across


def scatter_first(group, wire, mine, by_pair, by_ring, cut, name, step, across):
    if across:
        wire.put(
            mine(step, 1, 0), by_pair.at[step], group.device(0, 1), (name, "pair", step)
        )
    if step:
        wire.put(
            mine(step, across, 1),
            by_ring.at[4 - step, across],
            group.device(step, 0),
            (name, "ring", 4 - step, across),
        )


def scatter_steps(group, wire, mine, finish, last, buffers, name):
    by_pair, by_ring, by_ring_last, by_pair_last = buffers
    going, going_last = last
    for step in (1, 3, 2, 0):
        wire.got(by_pair.at[step], group.device(0, 1), (name, "pair", step))
        total = wide(mine(step, 0, 0)[...]) + wide(by_pair[step])
        if step:
            going[step] = total.astype(jnp.bfloat16)
            wire.put(
                going.at[step], by_ring_last.at[4 - step], group.device(step, 0),
                (name, "last", 4 - step),
            )
        else:
            first_total = total
    for across in (1, 0):
        total = wide(mine(0, across, 1)[...])
        for step in (1, 3, 2):
            wire.got(by_ring.at[step, across], group.device(step, 0), (name, "ring", step, across))
            total = total + wide(by_ring[step, across])
        if across:
            going_last[...] = total.astype(jnp.bfloat16)
            wire.put(going_last, by_pair_last, group.device(0, 1), (name, "last"))
    yield
    wire.got(by_pair_last, group.device(0, 1), (name, "last"))
    finish(1, total + wide(by_pair_last[...]))
    for step in (1, 3, 2):
        wire.got(by_ring_last.at[step], group.device(step, 0), (name, "last", step))
        first_total = first_total + wide(by_ring_last[step])
    finish(0, first_total)


def scatter_buffers(rows, columns, cut):
    first, second, kind = cut, rows - cut, jnp.bfloat16
    return [
        pltpu.VMEM((4, first, columns), kind),
        pltpu.VMEM((4, 2, second, columns), kind),
        pltpu.VMEM((4, first, columns), kind),
        pltpu.VMEM((second, columns), kind),
        pltpu.VMEM((4, first, columns), kind),
        pltpu.VMEM((second, columns), kind),
    ]


def part_of(half, rows, cut):
    return pl.ds(cut, rows - cut) if half else pl.ds(0, cut)


def chunk_views(ref, rows, cut):
    return lambda step, across, half: ref.at[step, across, part_of(half, rows, cut)]


def column_views(ref, rows, columns, cut):
    def view(slot, half):
        return ref.at[
            part_of(half, rows, cut), pl.ds(pl.multiple_of(slot * columns, columns), columns)
        ]

    return view


def row_views(ref, rows, cut):
    def view(slot, half):
        start, size = (cut, rows - cut) if half else (0, cut)
        return ref.at[pl.ds(pl.multiple_of(slot * rows + start, 32), size)]

    return view


def shard_views(ref, rows, cut):
    return lambda half: ref.at[part_of(half, rows, cut)]


def run(steps):
    for _ in steps:
        pass


def advance(steps):
    return next(steps, None)


ANYWHERE = pl.BlockSpec(memory_space=pl.ANY)
ON_CHIP = pl.BlockSpec(memory_space=pltpu.VMEM)


def dot(a, b, over=((1,), (0,))):
    return lax.dot_general(a, b, (over, ((), ())), preferred_element_type=jnp.float32)


BY_ROWS = ((1,), (1,))
BY_COLUMNS = ((0,), (0,))


def forward_kernel(
    source, row_token, stitch, gain, q_hbm, kv_hbm, o_hbm, out_grad,
    token_out, hidden_out, hidden, queries, pairs, squares, grad_context,
    send, recv, local, loads,
    stitch_in, q_in, kv_in, o_in, rows_in, hidden_in, gradient_in,
    product, token_part, token_rows, total_context,
    *buffers,
):
    tp, tok, wire = Group("tp"), Group("tok"), Wire(send, recv)
    rows, columns = out_grad.shape
    source_rows = source.shape[0]
    tiles = token_part.shape[0] // rows
    pulls = [
        pltpu.make_async_copy(a, b, loads.at[i])
        for i, (a, b) in enumerate(
            ((stitch, stitch_in), (o_hbm, o_in), (q_hbm, q_in), (kv_hbm, kv_in))
        )
    ]
    for pull in pulls:
        pull.start()
    greet(tp, tok)
    pulls[0].wait()

    def placed(tile, taken):
        index = lax.broadcasted_iota(jnp.int32, (rows, taken.shape[1]), 0) + tile * rows
        return jnp.where(index == taken, 1.0, 0.0).astype(jnp.bfloat16)

    def source_ready(step, across):
        block = tp.index(step, across) // 2
        here = pl.ds(pl.multiple_of(block * 2 * source_rows, 2 * source_rows), 2 * source_rows)
        product[...] = dot(rows_in[here, :], stitch_in[...]).astype(jnp.bfloat16)

        @pl.loop(0, tiles)
        def _(tile):
            there = pl.ds(pl.multiple_of(tile * rows, rows), rows)
            moved = dot(placed(tile, row_token[:, here]), product[...]).astype(jnp.bfloat16)
            if (step, across) == (0, 0):
                token_part[there, :] = moved
            else:
                token_part[there, :] = token_part[there, :] + moved

    def nothing(step, across):
        pass

    run(
        gather_steps(
            tp, wire, shard_views(source, source_rows, 64), row_views(rows_in, source_rows, 64),
            64, local.at[pl.ds(0, 2)], "source", source_ready,
        )
    )

    cut = 64
    going, buffers = buffers[4:], buffers[:4]

    def part(step, across, half):
        start, size = (cut, rows - cut) if half else (0, cut)
        return token_part.at[
            pl.ds(pl.multiple_of(tok.index(step, across) * rows + start, 32), size)
        ]

    def finish(half, value):
        hidden[part_of(half, rows, cut), :] = value.astype(hidden.dtype)

    for step, across in ORDER:
        scatter_first(tok, wire, part, buffers[0], buffers[1], cut, "hidden", step, across)
    gathering = gather_steps(
        tp, wire, shard_views(out_grad, rows, 192), column_views(gradient_in, rows, columns, 192),
        192, local.at[pl.ds(2, 2)], "gradient", nothing,
    )
    scattering = scatter_steps(tok, wire, part, finish, going, buffers, "hidden")

    def reorder(first, last):
        @pl.loop(first, last)
        def _(tile):
            there = pl.ds(pl.multiple_of(tile * rows, rows), rows)
            token_rows[there, :] = dot(placed(tile, row_token[...]), rows_in[...]).astype(
                token_rows.dtype
            )

    advance(gathering)
    reorder(0, tiles // 4)
    advance(scattering)
    advance(gathering)
    advance(gathering)
    reorder(tiles // 4, tiles // 2)
    advance(scattering)
    run(gathering)

    def hidden_ready(step, across):
        if (step, across) == (0, 0):
            pulls[2].wait()
            pulls[3].wait()
        block = tp.index(step, across) // 2
        here = pl.ds(pl.multiple_of(block * 2 * columns, 2 * columns), 2 * columns)
        value = wide(hidden_in[:, here])
        scaled = (value * gain[:, here]).astype(jnp.bfloat16)
        to_queries = dot(scaled, q_in[here, :])
        to_pairs = dot(scaled, kv_in[here, :])
        squared = jnp.broadcast_to(
            jnp.sum(value * value, axis=1, keepdims=True), squares.shape
        )
        if (step, across) == (0, 0):
            queries[...], pairs[...], squares[...] = to_queries, to_pairs, squared
        else:
            queries[...] += to_queries
            pairs[...] += to_pairs
            squares[...] += squared

    gathering = gather_steps(
        tp, wire, shard_views(hidden, rows, 128), column_views(hidden_in, rows, columns, 128),
        128, local.at[pl.ds(4, 2)], "all", hidden_ready,
    )
    advance(gathering)
    reorder(tiles // 2, tiles)
    tokens_out = pltpu.make_async_copy(token_rows, token_out, loads.at[4])
    tokens_out.start()
    advance(gathering)
    advance(gathering)
    pulls[1].wait()
    total_context[...] = jnp.zeros_like(total_context)

    @pl.loop(0, gradient_in.shape[1] // 1024)
    def _(block):
        here = pl.ds(pl.multiple_of(block * 1024, 1024), 1024)
        total_context[...] += dot(gradient_in[:, here], o_in[:, here], BY_ROWS)

    grad_context[...] = total_context[...].astype(grad_context.dtype)
    run(gathering)
    hidden_copy = pltpu.make_async_copy(hidden_in, hidden_out, loads.at[5])
    hidden_copy.start()
    tokens_out.wait()
    hidden_copy.wait()
    wire.drain()


def forward(source, row_token, stitch, gain, q_weight, kv_weight, o_weight, out_grad):
    rows, columns = out_grad.shape
    source_rows, features = source.shape
    tokens, width, heads = 16 * source_rows, 16 * columns, q_weight.shape[1]
    half = jnp.bfloat16
    return pl.pallas_call(
        forward_kernel,
        out_shape=(
            jax.ShapeDtypeStruct((tokens, features), half),
            jax.ShapeDtypeStruct((rows, width), half),
            jax.ShapeDtypeStruct((rows, columns), half),
            jax.ShapeDtypeStruct((rows, heads), jnp.float32),
            jax.ShapeDtypeStruct((rows, HD), jnp.float32),
            jax.ShapeDtypeStruct((rows, HD), jnp.float32),
            jax.ShapeDtypeStruct((rows, heads), half),
        ),
        in_specs=[ANYWHERE, ON_CHIP, ANYWHERE, ON_CHIP, ANYWHERE, ANYWHERE, ANYWHERE, ANYWHERE],
        out_specs=(ANYWHERE, ANYWHERE) + (ON_CHIP,) * 5,
        scratch_shapes=[
            pltpu.SemaphoreType.DMA((120,)),
            pltpu.SemaphoreType.DMA((120,)),
            pltpu.SemaphoreType.DMA((6,)),
            pltpu.SemaphoreType.DMA((6,)),
            pltpu.VMEM(stitch.shape, half),
            pltpu.VMEM(q_weight.shape, half),
            pltpu.VMEM(kv_weight.shape, half),
            pltpu.VMEM(o_weight.shape, half),
            pltpu.VMEM((tokens, features), half),
            pltpu.VMEM((rows, width), half),
            pltpu.VMEM((rows, width), half),
            pltpu.VMEM((2 * source_rows, columns), half),
            pltpu.VMEM((tokens, columns), half),
            pltpu.VMEM((tokens, features), half),
            pltpu.VMEM((rows, heads), jnp.float32),
        ]
        + scatter_buffers(rows, columns, 64),
        compiler_params=pltpu.CompilerParams(
            collective_id=1, has_side_effects=True, vmem_limit_bytes=60 << 20
        ),
        cost_estimate=pl.CostEstimate(flops=30 << 30, bytes_accessed=200 << 20, transcendentals=0),
        name="forward",
    )(
        source, row_token.reshape(1, -1), stitch, gain.reshape(1, -1), q_weight, kv_weight,
        o_weight, out_grad,
    )


def backward_kernel(
    queries, pairs, squares, grad_context, cosines, sines, seg_row, seg_column, gain,
    hidden, out_grad, hidden_hbm, token_hbm, q_hbm, kv_hbm, o_hbm,
    layer_out, stitch_grad,
    send, recv, local, loads,
    q_in, kv_in, o_in, hidden_in, token_rows, every_grad, grad_hidden,
    queries_in, context, grad_queries, grad_pairs, own_pair, other_pair, leaving_pair, back_pair,
    mine, leaving, by_core, mine_out, leaving_out, by_core_out,
    *buffers,
):
    tp, tok, wire = Group("tp"), Group("tok"), Wire(send, recv)
    rows, columns = out_grad.shape
    width = hidden_in.shape[1]
    half = jnp.bfloat16
    pulls = [
        pltpu.make_async_copy(a, b, loads.at[i])
        for i, (a, b) in enumerate(
            (
                (q_hbm, q_in), (kv_hbm, kv_in), (hidden_hbm, hidden_in), (o_hbm, o_in),
                (token_hbm, token_rows),
            )
        )
    ]
    for pull in pulls:
        pull.start()
    greet(tp, tok)

    cosine, sine = cosines[...], sines[...]

    def rotate(x):
        return x * cosine + pltpu.roll(x, HD // 2, 1) * sine

    def unrotate(x):
        return x * cosine - pltpu.roll(x, HD // 2, 1) * sine

    inv_rms = lax.rsqrt(squares[...] / width + epsilon)
    is_key = tp.core == 0
    sibling = tp.device(0, 0, 1)
    projected = pairs[...] * inv_rms
    own_pair[...] = jnp.where(is_key, rotate(projected), projected).astype(half)
    wire.put(own_pair, other_pair, sibling, "pair")
    heads = queries.shape[1] // HD
    for head in range(heads):
        lanes = pl.ds(head * HD, HD)
        queries_in[:, lanes] = rotate(queries[:, lanes] * inv_rms).astype(half)
    allowed = (seg_column[...] == seg_row[...]) & (
        lax.broadcasted_iota(jnp.int32, (rows, rows), 1)
        <= lax.broadcasted_iota(jnp.int32, (rows, rows), 0)
    )
    wire.got(other_pair, sibling, "pair")
    keys = jnp.where(is_key, own_pair[...], other_pair[...])
    values = jnp.where(is_key, other_pair[...], own_pair[...])
    scale = 1.0 / math.sqrt(HD)
    grad_keys = jnp.zeros((rows, HD), jnp.float32)
    grad_values = jnp.zeros((rows, HD), jnp.float32)
    along = jnp.zeros((rows, 1), jnp.float32)
    for head in range(heads):
        lanes = pl.ds(head * HD, HD)
        query, gradient = queries_in[:, lanes], grad_context[:, lanes]
        scores = jnp.where(allowed, dot(query, keys, BY_ROWS) * scale, -1e30)
        exponents = jnp.exp(scores - jnp.max(scores, axis=1, keepdims=True))
        attention = exponents / jnp.sum(exponents, axis=1, keepdims=True)
        attention_half = attention.astype(half)
        context[:, lanes] = dot(attention_half, values).astype(half)
        grad_probs = dot(gradient, values, BY_ROWS)
        centered = grad_probs - jnp.sum(grad_probs * attention, axis=1, keepdims=True)
        score_gradient = (attention * centered * scale).astype(half)
        grad_query = unrotate(dot(score_gradient, keys)).astype(half)
        grad_queries[:, lanes] = grad_query
        along = along + jnp.sum(wide(grad_query) * queries[:, lanes], axis=1, keepdims=True)
        grad_keys = grad_keys + dot(score_gradient, query, BY_COLUMNS)
        grad_values = grad_values + dot(attention_half, gradient, BY_COLUMNS)
    leaving_pair[...] = jnp.where(is_key, grad_values, grad_keys).astype(half)
    wire.put(leaving_pair, back_pair, sibling, "back")
    wire.got(back_pair, sibling, "back")
    summed = jnp.where(is_key, grad_keys, grad_values) + wide(back_pair[...])
    pair_gradient = jnp.where(is_key, unrotate(summed), summed).astype(half)
    grad_pairs[...] = pair_gradient
    along = along + jnp.sum(wide(pair_gradient) * pairs[...], axis=1, keepdims=True)
    inv = inv_rms[:, :1]
    pulled = inv * inv * inv * along / width
    for pull in pulls[:3]:
        pull.wait()

    def gradient_term(slot):
        here = pl.ds(pl.multiple_of(slot * columns, columns), columns)
        value = dot(grad_queries[...], q_in[here, :], BY_ROWS)
        value = value + dot(grad_pairs[...], kv_in[here, :], BY_ROWS)
        return (inv * (gain[:, here] * value) - wide(hidden_in[:, here]) * pulled).astype(half)

    def output_term(slot):
        here = pl.ds(pl.multiple_of(slot * columns, columns), columns)
        return dot(context[...], o_in[:, here]).astype(half)

    first, second = buffers[:6], buffers[6:]
    cut_first, cut_second = 128, 64
    mine_first = chunk_views(mine, rows, cut_first)
    mine_second = chunk_views(mine_out, rows, cut_second)

    def gradient_total(where, value):
        here = part_of(where, rows, cut_first)
        grad_hidden[here, :] = (wide(out_grad[here, :]) + value).astype(half)

    def output_total(where, value):
        here = part_of(where, rows, cut_second)
        layer_out[here, :] = (wide(hidden[here, :]) + value).astype(half)

    meeting = core_steps(tp, wire, gradient_term, mine, leaving, by_core, "gradient")
    advance(meeting)
    for count, (step, across) in enumerate(ORDER):
        advance(meeting)
        scatter_first(
            tp, wire, mine_first, first[0], first[1], cut_first, "gradient", step, across
        )
        advance(meeting)
    pulls[3].wait()
    run(core_steps(tp, wire, output_term, mine_out, leaving_out, by_core_out, "output"))
    scattering = scatter_steps(
        tp, wire, mine_first, gradient_total, first[4:], first[:4], "gradient"
    )
    advance(scattering)
    run(scattering)

    def pack_ready(step, across):
        here = pl.ds(pl.multiple_of(tok.index(step, across) * rows, rows), rows)
        value = dot(token_rows[here, :], every_grad[here, :], BY_COLUMNS)
        if (step, across) == (0, 0):
            stitch_grad[...] = value
        else:
            stitch_grad[...] += value

    cut_grad = 192
    gathering = gather_steps(
        tok, wire, shard_views(grad_hidden, rows, cut_grad), row_views(every_grad, rows, cut_grad),
        cut_grad, local, "every", pack_ready,
    )
    pulls[4].wait()
    advance(gathering)
    for step, across in ORDER:
        scatter_first(tp, wire, mine_second, second[0], second[1], cut_second, "output", step, across)
    scattering = scatter_steps(
        tp, wire, mine_second, output_total, second[4:], second[:4], "output"
    )
    advance(gathering)
    advance(gathering)
    advance(scattering)
    run(gathering)
    run(scattering)
    wire.drain()


def backward(
    queries, pairs, squares, grad_context, cosines, sines, seg_ids, gain, hidden, out_grad,
    hidden_all, token_rows, q_weight, kv_weight, o_weight,
):
    rows, columns = out_grad.shape
    tokens, features = token_rows.shape
    half = jnp.bfloat16
    chunks = pltpu.VMEM((4, 2, rows, columns), half)
    pair = pltpu.VMEM((rows, HD), half)
    wide_shape = pltpu.VMEM((rows, q_weight.shape[1]), half)
    return pl.pallas_call(
        backward_kernel,
        out_shape=(
            jax.ShapeDtypeStruct((rows, columns), half),
            jax.ShapeDtypeStruct((features, columns), jnp.float32),
        ),
        in_specs=[ON_CHIP] * 11 + [ANYWHERE] * 5,
        out_specs=(ON_CHIP, ON_CHIP),
        scratch_shapes=[
            pltpu.SemaphoreType.DMA((80,)),
            pltpu.SemaphoreType.DMA((80,)),
            pltpu.SemaphoreType.DMA((2,)),
            pltpu.SemaphoreType.DMA((5,)),
            pltpu.VMEM(q_weight.shape, half),
            pltpu.VMEM(kv_weight.shape, half),
            pltpu.VMEM(o_weight.shape, half),
            pltpu.VMEM(hidden_all.shape, half),
            pltpu.VMEM(token_rows.shape, half),
            pltpu.VMEM((tokens, columns), half),
            pltpu.VMEM((rows, columns), half),
            wide_shape, wide_shape, wide_shape, pair, pair, pair, pair, pair,
        ]
        + [chunks] * 6
        + scatter_buffers(rows, columns, 128)
        + scatter_buffers(rows, columns, 64),
        compiler_params=pltpu.CompilerParams(
            collective_id=2, has_side_effects=True, vmem_limit_bytes=60 << 20
        ),
        cost_estimate=pl.CostEstimate(flops=10 << 30, bytes_accessed=200 << 20, transcendentals=0),
        name="backward",
    )(
        queries, pairs, squares, grad_context, cosines, sines, seg_ids, seg_ids.reshape(rows, 1),
        gain.reshape(1, -1), hidden, out_grad, hidden_all, token_rows, q_weight, kv_weight,
        o_weight,
    )


def body(
    source, row_token, seg_ids, stitch_weight, norm_gain, q_weight, kv_weight, o_weight, out_grad
):
    seg_row = seg_ids[0]
    earlier = jnp.sum((seg_row[None, :] < seg_row[:, None]).astype(jnp.int32), axis=1)
    index_row = jnp.arange(seg_row.shape[0], dtype=jnp.int32)
    angles = (index_row - earlier).astype(jnp.float32)[:, None] * frequencies()[None, :]
    cosines, sines = jnp.cos(angles), jnp.sin(angles)
    cosines = jnp.concatenate([cosines, cosines], axis=1)
    sines = jnp.concatenate([-sines, sines], axis=1)
    token_rows, hidden_all, hidden, queries, pairs, squares, grad_context = forward(
        source, row_token, stitch_weight, norm_gain, q_weight, kv_weight, o_weight, out_grad
    )
    return backward(
        queries, pairs, squares, grad_context, cosines, sines, seg_ids, norm_gain, hidden,
        out_grad, hidden_all, token_rows, q_weight, kv_weight, o_weight,
    )


def solution(mesh):
    placed = (
        P("tp", "tok"),
        P(),
        P("tok", None),
        P("tok", "tp"),
        P(),
        P(None, "tp"),
        P(None, "tp"),
        P("tp", None),
        P("tok", "tp"),
    )
    return jax.shard_map(
        body,
        mesh=mesh,
        in_specs=placed,
        out_specs=(P("tok", "tp"), P("tok", "tp")),
        check_vma=False,
    )
```

time: 523 us -> 179 us (0.34)
  waiting for transfers between devices: 412 us -> 0 us
  Pallas kernels: 0 us -> 169 us
  matrix products: 50.8 us -> 0 us
  local copies, waits for them, and re-layouts: 25 us -> 6.22 us
  other arithmetic: 18.3 us -> 2.34 us
  between operations: 14.5 us -> 0.66 us
    all_gather x4 -> x0, waiting for transfers between devices: 209 us -> none  [the longest x1 57.1 us: body(): gradient_every_row = lax.all_gather(out_grad, 'tp', axis=1, tiled=True)]
    reduce_scatter x3 -> x0, waiting for transfers between devices: 201 us -> none  [the longest x1 82.1 us: body(): lax.psum_scatter(jnp.dot(context, o_weight, preferred_element_type=jnp.fl...]
    pallas_call x0 -> x2, Pallas kernels: none -> 169 us  [the longest x1 98.4 us: forward(): pl.pallas_call(forward_kernel, out_shape=(jax.ShapeDtypeStruct((tokens, f...]
    dot_general x14 -> x0, matrix products: 50.8 us -> none  [the longest x1 7.71 us: body(): jnp.dot(context, o_weight, preferred_element_type=jnp.float32)]
    gather x1 -> x0, local copies, waits for them, and re-layouts: 13.7 us -> none  [body(): token_rows = jnp.take(gathered, placing, axis=0)]
    convert_element_type x5 -> x0, other arithmetic: 10.2 us -> none  [the longest x1 5.84 us: body(): norm_term.astype(jnp.bfloat16)]
    scatter x1 -> x0, local copies, waits for them, and re-layouts: 8.04 us -> none  [body(): placing = jnp.zeros((every_row_stack,), jnp.int32).at[row_token].set(jnp....]
  transfers between devices with their start and end apart: 9 -> 0, of which waited for: 7 -> 0; matrix products, arithmetic and copies ran while one was open for 8% -> 0% of each run, Pallas kernels for 0% -> 0%
where the time goes in v2:
time: 179 us; the launch traced here: 178 us
  Pallas kernels  169 us (94%)
  local copies, waits for them, and re-layouts  6.22 us (3%)
  other arithmetic  2.34 us (1%)
    pallas_call x1, Pallas kernels, forward(): pl.pallas_call(forward_kernel, out_shape=(jax.ShapeDtypeStruct((tokens, f...  98.4 us
    pallas_call x1, Pallas kernels, backward(): pl.pallas_call(backward_kernel, out_shape=(jax.ShapeDtypeStruct((rows, co...  70.8 us
    unnamed x2, local copies, waits for them, and re-layouts  4.75 us

profile of v2, /device:TPU:0, one launch (start us, length us, event | category | flops | bytes accessed | tf_op | source)
XLA Modules:
  0.0 178.4 jit_solution(12989291296206792295)
XLA Ops:
  0.6 0.9 convert_reduce_fusion
  1.6 1.5 copy.12.seg_column
  3.1 0.5 fusion
  3.6 0.8 pad_maximum_fusion
  4.4 98.4 %forward.1 = (bf16[2048,1024]{1,0:T(8,128)(2,1)}, bf16[256,8192]{1,0:T(8,128)(2,1)}, bf16[256,512]{1,0:T(8,128)(2,1)}, f32[256,512]{1,0:T(8,128)}, f32[256,128]{...) custom-call(bf16[128,1024]{1,0:T(8,128)(2,1)} %source.1, s32[1,2048]{1,0:T(1,128)} %bitcast.8, ...), custom_call_target="tpu_custom_call" | custom-call | flops 32212254720 | bytes 209715200 | tf_op jit(solution)/shard_map/forward/pallas_call | solution.py:438
  102.8 70.8 %backward.1 = (bf16[256,512]{1,0:T(8,128)(2,1)}, f32[1024,512]{1,0:T(8,128)}) custom-call(f32[256,512]{1,0:T(8,128)} %get-tuple-element.9.queries, f32[256,128]{1,0:T(8,128)} %get-tuple-element.10.pairs, f32[256,128]{1,0:T(8,128)} %get-tuple-element.11.squares, bf16[256,512]{1,0:T(8,128)(2,1)} %get-tuple-element.12.grad_context, ...), custom_call_target="tpu_custom_call" | custom-call | flops 10737418240 | bytes 209715200 | tf_op jit(solution)/shard_map/backward/pallas_call | solution.py:641
  173.6 1.7 copy.15
  175.3 3.1 %copy.16 = f32[1024,512]{1,0:T(8,128)} copy(f32[1024,512]{1,0:T(8,128)} %get-tuple-element.24) | data formatting | bytes 4194304
  (2 shorter events, 0.0 us)

commit v3 on v2

--- a/solution.py
+++ b/solution.py
@@ -2,6 +2,7 @@
 
 import jax
 import jax.numpy as jnp
+import numpy as np
 from jax import lax
 from jax.experimental import pallas as pl
 from jax.experimental.pallas import tpu as pltpu
@@ -14,14 +15,17 @@
 
 
 def frequencies():
-    exponent = jnp.arange(0, HD, 2).astype(jnp.float32) / HD
-    plain_rate = 500000.0 ** (-exponent)
-    wavelength = 2.0 * math.pi / plain_rate
-    smoothing = (8192.0 / wavelength - 1.0) / 3.0
-    blended = (1.0 - smoothing) * plain_rate / 8.0 + smoothing * plain_rate
-    return jnp.where(
-        wavelength < 2048.0, plain_rate, jnp.where(wavelength > 8192.0, plain_rate / 8.0, blended)
-    )
+    exponent = np.arange(0, HD, 2, dtype=np.float32) / np.float32(HD)
+    plain_rate = np.power(np.float32(500000.0), -exponent)
+    wavelength = np.float32(2.0 * math.pi) / plain_rate
+    smoothing = (np.float32(8192.0) / wavelength - np.float32(1.0)) / np.float32(3.0)
+    blended = (np.float32(1.0) - smoothing) * plain_rate / np.float32(8.0) + smoothing * plain_rate
+    rate = np.where(
+        wavelength < 2048.0,
+        plain_rate,
+        np.where(wavelength > 8192.0, plain_rate / np.float32(8.0), blended),
+    )
+    return np.concatenate([rate, rate]).astype(np.float32)
 
 
 class Group:
@@ -84,14 +88,14 @@
             copy.wait_send()
 
 
-def greet(*groups):
+def announce(*groups):
     barrier = pltpu.get_barrier_semaphore()
     peers = [peer for group in groups for peer in group.peers()]
     for peer in peers:
         pl.semaphore_signal(
             barrier, inc=1, device_id=peer, device_id_type=pl.DeviceIdType.MESH
         )
-    pl.semaphore_wait(barrier, len(peers))
+    return lambda: pl.semaphore_wait(barrier, len(peers))
 
 
 def wide(value):
@@ -119,11 +123,15 @@
 
     own = group.index(0, 0)
     wire.put(shard(0), whole(own, 0), group.device(0, 1), (name, 0, 1, 0))
-    for half in (1, 0):
+
+    def along(half):
         for step in (1, 3, 2):
             wire.put(
                 shard(half), whole(own, half), group.device(step, 0), (name, 4 - step, 0, half)
             )
+
+    along(1)
+    along(0)
     wire.put(shard(1), whole(own, 1), group.device(0, 1), (name, 0, 1, 1))
     kept = [pltpu.make_async_copy(shard(half), whole(own, half), local.at[half]) for half in (0, 1)]
     for copy in kept:
@@ -135,8 +143,8 @@
             )
     for copy in kept:
         copy.wait()
+    yield
     complete(0, 0)
-    yield
     arrived(0, 1, 0)
     view = whole(group.index(0, 1), 0)
     for step in (1, 3, 2):
@@ -313,40 +321,65 @@
             ((stitch, stitch_in), (o_hbm, o_in), (q_hbm, q_in), (kv_hbm, kv_in))
         )
     ]
+    met = announce(tp, tok)
     for pull in pulls:
         pull.start()
-    greet(tp, tok)
+    met()
     pulls[0].wait()
 
-    def placed(tile, taken):
-        index = lax.broadcasted_iota(jnp.int32, (rows, taken.shape[1]), 0) + tile * rows
+    def placed(tile, taken, size=rows):
+        index = lax.broadcasted_iota(jnp.int32, (size, taken.shape[1]), 0) + tile * size
         return jnp.where(index == taken, 1.0, 0.0).astype(jnp.bfloat16)
 
+    def block_of(step, across):
+        block = tp.index(step, across) // 2
+        return pl.ds(pl.multiple_of(block * 2 * source_rows, 2 * source_rows), 2 * source_rows)
+
+    def tile_of(tile, size=rows):
+        return pl.ds(pl.multiple_of(tile * size, size), size)
+
+    late = [(1, 1), (3, 1), (2, 1)]
+
     def source_ready(step, across):
-        block = tp.index(step, across) // 2
-        here = pl.ds(pl.multiple_of(block * 2 * source_rows, 2 * source_rows), 2 * source_rows)
-        product[...] = dot(rows_in[here, :], stitch_in[...]).astype(jnp.bfloat16)
-
-        @pl.loop(0, tiles)
+        here = block_of(step, across)
+        slot = late.index((step, across)) if (step, across) in late else 0
+        product[slot] = dot(rows_in[here, :], stitch_in[...]).astype(jnp.bfloat16)
+        if (step, across) in late:
+            return
+
+        @pl.loop(0, tiles // 4)
         def _(tile):
-            there = pl.ds(pl.multiple_of(tile * rows, rows), rows)
-            moved = dot(placed(tile, row_token[:, here]), product[...]).astype(jnp.bfloat16)
+            there = tile_of(tile, 4 * rows)
+            moved = dot(placed(tile, row_token[:, here], 4 * rows), product[0]).astype(
+                jnp.bfloat16
+            )
             if (step, across) == (0, 0):
                 token_part[there, :] = moved
             else:
                 token_part[there, :] = token_part[there, :] + moved
 
+    def place_late(tile):
+        total = wide(token_part[tile_of(tile), :])
+        for slot, (step, across) in enumerate(late):
+            total = total + dot(placed(tile, row_token[:, block_of(step, across)]), product[slot])
+        token_part[tile_of(tile), :] = total.astype(jnp.bfloat16)
+
     def nothing(step, across):
         pass
 
-    run(
-        gather_steps(
-            tp, wire, shard_views(source, source_rows, 64), row_views(rows_in, source_rows, 64),
-            64, local.at[pl.ds(0, 2)], "source", source_ready,
-        )
-    )
-
-    cut = 64
+    fetching = gather_steps(
+        tp, wire, shard_views(source, source_rows, 64), row_views(rows_in, source_rows, 64),
+        64, local.at[pl.ds(0, 2)], "source", source_ready,
+    )
+    gathering = gather_steps(
+        tp, wire, shard_views(out_grad, rows, 192), column_views(gradient_in, rows, columns, 192),
+        192, local.at[pl.ds(2, 2)], "gradient", nothing,
+    )
+    for _ in range(3):
+        advance(fetching)
+    advance(gathering)
+    run(fetching)
+    cut = 128
     going, buffers = buffers[4:], buffers[:4]
 
     def part(step, across, half):
@@ -359,36 +392,30 @@
         hidden[part_of(half, rows, cut), :] = value.astype(hidden.dtype)
 
     for step, across in ORDER:
+        place_late(tok.index(step, across))
         scatter_first(tok, wire, part, buffers[0], buffers[1], cut, "hidden", step, across)
-    gathering = gather_steps(
-        tp, wire, shard_views(out_grad, rows, 192), column_views(gradient_in, rows, columns, 192),
-        192, local.at[pl.ds(2, 2)], "gradient", nothing,
-    )
     scattering = scatter_steps(tok, wire, part, finish, going, buffers, "hidden")
 
     def reorder(first, last):
-        @pl.loop(first, last)
+        @pl.loop(first // 2, last // 2)
         def _(tile):
-            there = pl.ds(pl.multiple_of(tile * rows, rows), rows)
-            token_rows[there, :] = dot(placed(tile, row_token[...]), rows_in[...]).astype(
+            token_rows[tile_of(tile, 2 * rows), :] = dot(
+                placed(tile, row_token[...], 2 * rows), rows_in[...]
+            ).astype(
                 token_rows.dtype
             )
 
-    advance(gathering)
-    reorder(0, tiles // 4)
+    reorder(0, tiles // 2)
     advance(scattering)
     advance(gathering)
-    advance(gathering)
-    reorder(tiles // 4, tiles // 2)
     advance(scattering)
-    run(gathering)
-
     def hidden_ready(step, across):
         if (step, across) == (0, 0):
             pulls[2].wait()
             pulls[3].wait()
-        block = tp.index(step, across) // 2
-        here = pl.ds(pl.multiple_of(block * 2 * columns, 2 * columns), 2 * columns)
+        here = pl.ds(
+            pl.multiple_of(tp.index(step, across) // 2 * 2 * columns, 2 * columns), 2 * columns
+        )
         value = wide(hidden_in[:, here])
         scaled = (value * gain[:, here]).astype(jnp.bfloat16)
         to_queries = dot(scaled, q_in[here, :])
@@ -403,17 +430,20 @@
             pairs[...] += to_pairs
             squares[...] += squared
 
-    gathering = gather_steps(
+    collecting = gather_steps(
         tp, wire, shard_views(hidden, rows, 128), column_views(hidden_in, rows, columns, 128),
         128, local.at[pl.ds(4, 2)], "all", hidden_ready,
     )
-    advance(gathering)
-    reorder(tiles // 2, tiles)
+    advance(collecting)
+    run(gathering)
+    reorder(tiles // 2, tiles * 3 // 4)
+    advance(collecting)
+    reorder(tiles * 3 // 4, tiles)
     tokens_out = pltpu.make_async_copy(token_rows, token_out, loads.at[4])
     tokens_out.start()
-    advance(gathering)
-    advance(gathering)
+    advance(collecting)
     pulls[1].wait()
+    advance(collecting)
     total_context[...] = jnp.zeros_like(total_context)
 
     @pl.loop(0, gradient_in.shape[1] // 1024)
@@ -422,7 +452,7 @@
         total_context[...] += dot(gradient_in[:, here], o_in[:, here], BY_ROWS)
 
     grad_context[...] = total_context[...].astype(grad_context.dtype)
-    run(gathering)
+    run(collecting)
     hidden_copy = pltpu.make_async_copy(hidden_in, hidden_out, loads.at[5])
     hidden_copy.start()
     tokens_out.wait()
@@ -460,12 +490,12 @@
             pltpu.VMEM((tokens, features), half),
             pltpu.VMEM((rows, width), half),
             pltpu.VMEM((rows, width), half),
-            pltpu.VMEM((2 * source_rows, columns), half),
+            pltpu.VMEM((3, 2 * source_rows, columns), half),
             pltpu.VMEM((tokens, columns), half),
             pltpu.VMEM((tokens, features), half),
             pltpu.VMEM((rows, heads), jnp.float32),
         ]
-        + scatter_buffers(rows, columns, 64),
+        + scatter_buffers(rows, columns, 128),
         compiler_params=pltpu.CompilerParams(
             collective_id=1, has_side_effects=True, vmem_limit_bytes=60 << 20
         ),
@@ -478,7 +508,7 @@
 
 
 def backward_kernel(
-    queries, pairs, squares, grad_context, cosines, sines, seg_row, seg_column, gain,
+    queries, pairs, squares, grad_context, rates, seg_row, gain,
     hidden, out_grad, hidden_hbm, token_hbm, q_hbm, kv_hbm, o_hbm,
     layer_out, stitch_grad,
     send, recv, local, loads,
@@ -500,11 +530,21 @@
             )
         )
     ]
+    met = announce(tp, tok)
     for pull in pulls:
         pull.start()
-    greet(tp, tok)
-
-    cosine, sine = cosines[...], sines[...]
+    segments = jnp.broadcast_to(seg_row[...].astype(jnp.float32), (rows, rows))
+    own_segment = segments.T
+    index = lax.broadcasted_iota(jnp.int32, (rows, rows), 0)
+    allowed = (own_segment == segments) & (
+        lax.broadcasted_iota(jnp.int32, (rows, rows), 1) <= index
+    )
+    earlier = jnp.sum(jnp.where(segments < own_segment, 1.0, 0.0), axis=1, keepdims=True)
+    angles = (index[:, :HD].astype(jnp.float32) - earlier) * rates[...]
+    cosine, sine = jnp.cos(angles), jnp.sin(angles)
+    sine = jnp.where(
+        lax.broadcasted_iota(jnp.int32, (rows, HD), 1) < HD // 2, -sine, sine
+    )
 
     def rotate(x):
         return x * cosine + pltpu.roll(x, HD // 2, 1) * sine
@@ -517,15 +557,12 @@
     sibling = tp.device(0, 0, 1)
     projected = pairs[...] * inv_rms
     own_pair[...] = jnp.where(is_key, rotate(projected), projected).astype(half)
+    heads = queries.shape[1] // HD
+    met()
     wire.put(own_pair, other_pair, sibling, "pair")
-    heads = queries.shape[1] // HD
     for head in range(heads):
         lanes = pl.ds(head * HD, HD)
         queries_in[:, lanes] = rotate(queries[:, lanes] * inv_rms).astype(half)
-    allowed = (seg_column[...] == seg_row[...]) & (
-        lax.broadcasted_iota(jnp.int32, (rows, rows), 1)
-        <= lax.broadcasted_iota(jnp.int32, (rows, rows), 0)
-    )
     wire.got(other_pair, sibling, "pair")
     keys = jnp.where(is_key, own_pair[...], other_pair[...])
     values = jnp.where(is_key, other_pair[...], own_pair[...])
@@ -629,7 +666,7 @@
 
 
 def backward(
-    queries, pairs, squares, grad_context, cosines, sines, seg_ids, gain, hidden, out_grad,
+    queries, pairs, squares, grad_context, seg_ids, gain, hidden, out_grad,
     hidden_all, token_rows, q_weight, kv_weight, o_weight,
 ):
     rows, columns = out_grad.shape
@@ -644,7 +681,7 @@
             jax.ShapeDtypeStruct((rows, columns), half),
             jax.ShapeDtypeStruct((features, columns), jnp.float32),
         ),
-        in_specs=[ON_CHIP] * 11 + [ANYWHERE] * 5,
+        in_specs=[ON_CHIP] * 9 + [ANYWHERE] * 5,
         out_specs=(ON_CHIP, ON_CHIP),
         scratch_shapes=[
             pltpu.SemaphoreType.DMA((80,)),
@@ -669,7 +706,7 @@
         cost_estimate=pl.CostEstimate(flops=10 << 30, bytes_accessed=200 << 20, transcendentals=0),
         name="backward",
     )(
-        queries, pairs, squares, grad_context, cosines, sines, seg_ids, seg_ids.reshape(rows, 1),
+        queries, pairs, squares, grad_context, jnp.asarray(frequencies())[None], seg_ids,
         gain.reshape(1, -1), hidden, out_grad, hidden_all, token_rows, q_weight, kv_weight,
         o_weight,
     )
@@ -678,18 +715,11 @@
 def body(
     source, row_token, seg_ids, stitch_weight, norm_gain, q_weight, kv_weight, o_weight, out_grad
 ):
-    seg_row = seg_ids[0]
-    earlier = jnp.sum((seg_row[None, :] < seg_row[:, None]).astype(jnp.int32), axis=1)
-    index_row = jnp.arange(seg_row.shape[0], dtype=jnp.int32)
-    angles = (index_row - earlier).astype(jnp.float32)[:, None] * frequencies()[None, :]
-    cosines, sines = jnp.cos(angles), jnp.sin(angles)
-    cosines = jnp.concatenate([cosines, cosines], axis=1)
-    sines = jnp.concatenate([-sines, sines], axis=1)
     token_rows, hidden_all, hidden, queries, pairs, squares, grad_context = forward(
         source, row_token, stitch_weight, norm_gain, q_weight, kv_weight, o_weight, out_grad
     )
     return backward(
-        queries, pairs, squares, grad_context, cosines, sines, seg_ids, norm_gain, hidden,
+        queries, pairs, squares, grad_context, seg_ids, norm_gain, hidden,
         out_grad, hidden_all, token_rows, q_weight, kv_weight, o_weight,
     )
 

time: 179 us -> 160 us (0.89)
  Pallas kernels: 169 us -> 154 us
  other arithmetic: 2.34 us -> 0 us
    pallas_call x1, Pallas kernels: 98.4 us -> 82.2 us  [forward(): pl.pallas_call(forward_kernel, out_shape=(jax.ShapeDtypeStruct((tokens, f...]
where the time goes in v3:
time: 160 us; the launch traced here: 159 us
  Pallas kernels  154 us (96%)
  local copies, waits for them, and re-layouts  4.75 us (3%)
    pallas_call x1, Pallas kernels, forward(): pl.pallas_call(forward_kernel, out_shape=(jax.ShapeDtypeStruct((tokens, f...  82.2 us
    pallas_call x1, Pallas kernels, backward(): pl.pallas_call(backward_kernel, out_shape=(jax.ShapeDtypeStruct((rows, co...  71.8 us
    unnamed x2, local copies, waits for them, and re-layouts  4.75 us

profile of v3, /device:TPU:0, one launch (start us, length us, event | category | flops | bytes accessed | tf_op | source)
XLA Modules:
  0.0 159.4 jit_solution(8722844160185532974)
XLA Ops:
  0.6 82.2 %forward.1 = (bf16[2048,1024]{1,0:T(8,128)(2,1)}, bf16[256,8192]{1,0:T(8,128)(2,1)}, bf16[256,512]{1,0:T(8,128)(2,1)}, f32[256,512]{1,0:T(8,128)}, f32[256,128]{...) custom-call(bf16[128,1024]{1,0:T(8,128)(2,1)} %source.1, s32[1,2048]{1,0:T(1,128)} %bitcast.4, ...), custom_call_target="tpu_custom_call" | custom-call | flops 32212254720 | bytes 209715200 | tf_op jit(solution)/shard_map/forward/pallas_call | solution.py:468
  82.9 71.8 %backward.1 = (bf16[256,512]{1,0:T(8,128)(2,1)}, f32[1024,512]{1,0:T(8,128)}) custom-call(f32[256,512]{1,0:T(8,128)} %get-tuple-element.9.queries, f32[256,128]{1,0:T(8,128)} %get-tuple-element.10.pairs, f32[256,128]{1,0:T(8,128)} %get-tuple-element.11.squares, bf16[256,512]{1,0:T(8,128)(2,1)} %get-tuple-element.12.grad_context, f32[1,128]{1,0:T(1,128)} %constant.4.rates, ...), custom_call_target="tpu_custom_call" | custom-call | flops 10737418240 | bytes 209715200 | tf_op jit(solution)/shard_map/backward/pallas_call | solution.py:678
  154.7 1.7 %copy.14 = bf16[256,512]{1,0:T(8,128)(2,1)} copy(bf16[256,512]{1,0:T(8,128)(2,1)} %get-tuple-element.18) | data formatting | bytes 524288
  156.4 3.1 %copy.15 = f32[1024,512]{1,0:T(8,128)} copy(f32[1024,512]{1,0:T(8,128)} %get-tuple-element.19) | data formatting | bytes 4194304

commit v4 on v3

--- a/solution.py
+++ b/solution.py
@@ -56,7 +56,7 @@
 
 class Wire:
     def __init__(self, send, recv):
-        self.send, self.recv, self.slots, self.sent = send, recv, {}, []
+        self.send, self.recv, self.slots, self.sent, self.waited = send, recv, {}, [], 0
 
     def slot(self, key):
         return self.recv.at[self.slots.setdefault(key, len(self.slots))]
@@ -84,8 +84,9 @@
         ).wait_recv()
 
     def drain(self):
-        for copy in self.sent:
+        for copy in self.sent[self.waited :]:
             copy.wait_send()
+        self.waited = len(self.sent)
 
 
 def announce(*groups):
@@ -180,19 +181,15 @@
 
 def core_steps(group, wire, term, mine, leaving, by_core, name):
     for step, across in ORDER:
-        leaving[step, across] = term(group.index(step, across, 1))
+        going, kept = leaving(step, across), mine(step, across)
+        going[...] = term(group.index(step, across, 1))
         wire.put(
-            leaving.at[step, across],
-            by_core.at[step, across],
-            group.device(0, 0, 1),
-            (name, "core", step, across),
-        )
-        mine[step, across] = term(group.index(step, across))
+            going, by_core.at[step, across], group.device(0, 0, 1), (name, "core", step, across)
+        )
+        kept[...] = term(group.index(step, across))
         yield
         wire.got(by_core.at[step, across], group.device(0, 0, 1), (name, "core", step, across))
-        mine[step, across] = (wide(mine[step, across]) + wide(by_core[step, across])).astype(
-            jnp.bfloat16
-        )
+        kept[...] = (wide(kept[...]) + wide(by_core[step, across])).astype(jnp.bfloat16)
         yield step, across
 
 
@@ -257,8 +254,20 @@
     return pl.ds(cut, rows - cut) if half else pl.ds(0, cut)
 
 
-def chunk_views(ref, rows, cut):
-    return lambda step, across, half: ref.at[step, across, part_of(half, rows, cut)]
+def chunks_in_rows(ref, rows, columns, side):
+    def view(step, across, half=None, cut=0):
+        start, size = (0, rows) if half is None else (cut, rows - cut) if half else (0, cut)
+        return ref.at[pl.ds((step * 2 + across) * rows + start, size), pl.ds(side * columns, columns)]
+
+    return view
+
+
+def chunks_in_columns(ref, rows, columns, side):
+    def view(step, across, half=None, cut=0):
+        part = pl.ds(0, rows) if half is None else part_of(half, rows, cut)
+        return ref.at[part, pl.ds((side * 8 + step * 2 + across) * columns, columns)]
+
+    return view
 
 
 def column_views(ref, rows, columns, cut):
@@ -303,12 +312,15 @@
 BY_COLUMNS = ((0,), (0,))
 
 
-def forward_kernel(
-    source, row_token, stitch, gain, q_hbm, kv_hbm, o_hbm, out_grad,
-    token_out, hidden_out, hidden, queries, pairs, squares, grad_context,
+def step_kernel(
+    source, row_token, seg_row, rates, stitch, gain, q_hbm, kv_hbm, o_hbm, out_grad,
+    layer_out, stitch_grad,
     send, recv, local, loads,
     stitch_in, q_in, kv_in, o_in, rows_in, hidden_in, gradient_in,
-    product, token_part, token_rows, total_context,
+    token_part, token_rows, hidden, queries, pairs, squares, grad_context,
+    cosines, sines, every_grad, grad_hidden,
+    queries_in, context, grad_queries, grad_pairs, own_pair, other_pair, leaving_pair, back_pair,
+    by_core, by_core_out,
     *buffers,
 ):
     tp, tok, wire = Group("tp"), Group("tok"), Wire(send, recv)
@@ -318,12 +330,23 @@
     pulls = [
         pltpu.make_async_copy(a, b, loads.at[i])
         for i, (a, b) in enumerate(
-            ((stitch, stitch_in), (o_hbm, o_in), (q_hbm, q_in), (kv_hbm, kv_in))
+            ((stitch, stitch_in), (o_hbm, o_in), (q_hbm, q_in), (kv_hbm, kv_in), (out_grad, grad_hidden))
         )
     ]
     met = announce(tp, tok)
     for pull in pulls:
         pull.start()
+    width, half = hidden_in.shape[1], jnp.bfloat16
+    segments = jnp.broadcast_to(seg_row[...].astype(jnp.float32), (rows, rows))
+    own_segment = segments.T
+    index = lax.broadcasted_iota(jnp.int32, (rows, rows), 0)
+    earlier = jnp.sum(jnp.where(segments < own_segment, 1.0, 0.0), axis=1, keepdims=True)
+    angles = (index[:, :HD].astype(jnp.float32) - earlier) * rates[...]
+    cosines[...] = jnp.cos(angles)
+    sine = jnp.sin(angles)
+    sines[...] = jnp.where(
+        lax.broadcasted_iota(jnp.int32, (rows, HD), 1) < HD // 2, -sine, sine
+    )
     met()
     pulls[0].wait()
 
@@ -339,18 +362,20 @@
         return pl.ds(pl.multiple_of(tile * size, size), size)
 
     late = [(1, 1), (3, 1), (2, 1)]
+    product = [queries_in, context, grad_queries]
+    total_context = stitch_grad.at[pl.ds(0, rows)]
 
     def source_ready(step, across):
         here = block_of(step, across)
         slot = late.index((step, across)) if (step, across) in late else 0
-        product[slot] = dot(rows_in[here, :], stitch_in[...]).astype(jnp.bfloat16)
+        product[slot][...] = dot(rows_in[here, :], stitch_in[...]).astype(jnp.bfloat16)
         if (step, across) in late:
             return
 
         @pl.loop(0, tiles // 4)
         def _(tile):
             there = tile_of(tile, 4 * rows)
-            moved = dot(placed(tile, row_token[:, here], 4 * rows), product[0]).astype(
+            moved = dot(placed(tile, row_token[:, here], 4 * rows), product[0][...]).astype(
                 jnp.bfloat16
             )
             if (step, across) == (0, 0):
@@ -361,7 +386,7 @@
     def place_late(tile):
         total = wide(token_part[tile_of(tile), :])
         for slot, (step, across) in enumerate(late):
-            total = total + dot(placed(tile, row_token[:, block_of(step, across)]), product[slot])
+            total = total + dot(placed(tile, row_token[:, block_of(step, across)]), product[slot][...])
         token_part[tile_of(tile), :] = total.astype(jnp.bfloat16)
 
     def nothing(step, across):
@@ -380,7 +405,7 @@
     advance(gathering)
     run(fetching)
     cut = 128
-    going, buffers = buffers[4:], buffers[:4]
+    later, going, buffers = buffers[6:], buffers[4:6], buffers[:4]
 
     def part(step, across, half):
         start, size = (cut, rows - cut) if half else (0, cut)
@@ -413,6 +438,7 @@
         if (step, across) == (0, 0):
             pulls[2].wait()
             pulls[3].wait()
+            pulls[4].wait()
         here = pl.ds(
             pl.multiple_of(tp.index(step, across) // 2 * 2 * columns, 2 * columns), 2 * columns
         )
@@ -439,8 +465,6 @@
     reorder(tiles // 2, tiles * 3 // 4)
     advance(collecting)
     reorder(tiles * 3 // 4, tiles)
-    tokens_out = pltpu.make_async_copy(token_rows, token_out, loads.at[4])
-    tokens_out.start()
     advance(collecting)
     pulls[1].wait()
     advance(collecting)
@@ -453,97 +477,13 @@
 
     grad_context[...] = total_context[...].astype(grad_context.dtype)
     run(collecting)
-    hidden_copy = pltpu.make_async_copy(hidden_in, hidden_out, loads.at[5])
-    hidden_copy.start()
-    tokens_out.wait()
-    hidden_copy.wait()
     wire.drain()
 
-
-def forward(source, row_token, stitch, gain, q_weight, kv_weight, o_weight, out_grad):
-    rows, columns = out_grad.shape
-    source_rows, features = source.shape
-    tokens, width, heads = 16 * source_rows, 16 * columns, q_weight.shape[1]
-    half = jnp.bfloat16
-    return pl.pallas_call(
-        forward_kernel,
-        out_shape=(
-            jax.ShapeDtypeStruct((tokens, features), half),
-            jax.ShapeDtypeStruct((rows, width), half),
-            jax.ShapeDtypeStruct((rows, columns), half),
-            jax.ShapeDtypeStruct((rows, heads), jnp.float32),
-            jax.ShapeDtypeStruct((rows, HD), jnp.float32),
-            jax.ShapeDtypeStruct((rows, HD), jnp.float32),
-            jax.ShapeDtypeStruct((rows, heads), half),
-        ),
-        in_specs=[ANYWHERE, ON_CHIP, ANYWHERE, ON_CHIP, ANYWHERE, ANYWHERE, ANYWHERE, ANYWHERE],
-        out_specs=(ANYWHERE, ANYWHERE) + (ON_CHIP,) * 5,
-        scratch_shapes=[
-            pltpu.SemaphoreType.DMA((120,)),
-            pltpu.SemaphoreType.DMA((120,)),
-            pltpu.SemaphoreType.DMA((6,)),
-            pltpu.SemaphoreType.DMA((6,)),
-            pltpu.VMEM(stitch.shape, half),
-            pltpu.VMEM(q_weight.shape, half),
-            pltpu.VMEM(kv_weight.shape, half),
-            pltpu.VMEM(o_weight.shape, half),
-            pltpu.VMEM((tokens, features), half),
-            pltpu.VMEM((rows, width), half),
-            pltpu.VMEM((rows, width), half),
-            pltpu.VMEM((3, 2 * source_rows, columns), half),
-            pltpu.VMEM((tokens, columns), half),
-            pltpu.VMEM((tokens, features), half),
-            pltpu.VMEM((rows, heads), jnp.float32),
-        ]
-        + scatter_buffers(rows, columns, 128),
-        compiler_params=pltpu.CompilerParams(
-            collective_id=1, has_side_effects=True, vmem_limit_bytes=60 << 20
-        ),
-        cost_estimate=pl.CostEstimate(flops=30 << 30, bytes_accessed=200 << 20, transcendentals=0),
-        name="forward",
-    )(
-        source, row_token.reshape(1, -1), stitch, gain.reshape(1, -1), q_weight, kv_weight,
-        o_weight, out_grad,
-    )
-
-
-def backward_kernel(
-    queries, pairs, squares, grad_context, rates, seg_row, gain,
-    hidden, out_grad, hidden_hbm, token_hbm, q_hbm, kv_hbm, o_hbm,
-    layer_out, stitch_grad,
-    send, recv, local, loads,
-    q_in, kv_in, o_in, hidden_in, token_rows, every_grad, grad_hidden,
-    queries_in, context, grad_queries, grad_pairs, own_pair, other_pair, leaving_pair, back_pair,
-    mine, leaving, by_core, mine_out, leaving_out, by_core_out,
-    *buffers,
-):
-    tp, tok, wire = Group("tp"), Group("tok"), Wire(send, recv)
-    rows, columns = out_grad.shape
-    width = hidden_in.shape[1]
-    half = jnp.bfloat16
-    pulls = [
-        pltpu.make_async_copy(a, b, loads.at[i])
-        for i, (a, b) in enumerate(
-            (
-                (q_hbm, q_in), (kv_hbm, kv_in), (hidden_hbm, hidden_in), (o_hbm, o_in),
-                (token_hbm, token_rows),
-            )
-        )
-    ]
-    met = announce(tp, tok)
-    for pull in pulls:
-        pull.start()
+    cosine, sine = cosines[...], sines[...]
     segments = jnp.broadcast_to(seg_row[...].astype(jnp.float32), (rows, rows))
-    own_segment = segments.T
-    index = lax.broadcasted_iota(jnp.int32, (rows, rows), 0)
-    allowed = (own_segment == segments) & (
-        lax.broadcasted_iota(jnp.int32, (rows, rows), 1) <= index
-    )
-    earlier = jnp.sum(jnp.where(segments < own_segment, 1.0, 0.0), axis=1, keepdims=True)
-    angles = (index[:, :HD].astype(jnp.float32) - earlier) * rates[...]
-    cosine, sine = jnp.cos(angles), jnp.sin(angles)
-    sine = jnp.where(
-        lax.broadcasted_iota(jnp.int32, (rows, HD), 1) < HD // 2, -sine, sine
+    allowed = (segments.T == segments) & (
+        lax.broadcasted_iota(jnp.int32, (rows, rows), 1)
+        <= lax.broadcasted_iota(jnp.int32, (rows, rows), 0)
     )
 
     def rotate(x):
@@ -558,7 +498,6 @@
     projected = pairs[...] * inv_rms
     own_pair[...] = jnp.where(is_key, rotate(projected), projected).astype(half)
     heads = queries.shape[1] // HD
-    met()
     wire.put(own_pair, other_pair, sibling, "pair")
     for head in range(heads):
         lanes = pl.ds(head * HD, HD)
@@ -595,8 +534,6 @@
     along = along + jnp.sum(wide(pair_gradient) * pairs[...], axis=1, keepdims=True)
     inv = inv_rms[:, :1]
     pulled = inv * inv * inv * along / width
-    for pull in pulls[:3]:
-        pull.wait()
 
     def gradient_term(slot):
         here = pl.ds(pl.multiple_of(slot * columns, columns), columns)
@@ -608,14 +545,23 @@
         here = pl.ds(pl.multiple_of(slot * columns, columns), columns)
         return dot(context[...], o_in[:, here]).astype(half)
 
-    first, second = buffers[:6], buffers[6:]
+    first, second = later[:6], later[6:]
     cut_first, cut_second = 128, 64
-    mine_first = chunk_views(mine, rows, cut_first)
-    mine_second = chunk_views(mine_out, rows, cut_second)
+    mine, leaving = (chunks_in_rows(rows_in, rows, columns, side) for side in (0, 1))
+    mine_out, leaving_out = (
+        chunks_in_columns(gradient_in, rows, columns, side) for side in (0, 1)
+    )
+
+    def mine_first(step, across, half):
+        return mine(step, across, half, cut_first)
+
+    def mine_second(step, across, half):
+        return mine_out(step, across, half, cut_second)
+
 
     def gradient_total(where, value):
         here = part_of(where, rows, cut_first)
-        grad_hidden[here, :] = (wide(out_grad[here, :]) + value).astype(half)
+        grad_hidden[here, :] = (wide(grad_hidden[here, :]) + value).astype(half)
 
     def output_total(where, value):
         here = part_of(where, rows, cut_second)
@@ -629,7 +575,6 @@
             tp, wire, mine_first, first[0], first[1], cut_first, "gradient", step, across
         )
         advance(meeting)
-    pulls[3].wait()
     run(core_steps(tp, wire, output_term, mine_out, leaving_out, by_core_out, "output"))
     scattering = scatter_steps(
         tp, wire, mine_first, gradient_total, first[4:], first[:4], "gradient"
@@ -648,9 +593,8 @@
     cut_grad = 192
     gathering = gather_steps(
         tok, wire, shard_views(grad_hidden, rows, cut_grad), row_views(every_grad, rows, cut_grad),
-        cut_grad, local, "every", pack_ready,
-    )
-    pulls[4].wait()
+        cut_grad, local.at[pl.ds(6, 2)], "every", pack_ready,
+    )
     advance(gathering)
     for step, across in ORDER:
         scatter_first(tp, wire, mine_second, second[0], second[1], cut_second, "output", step, across)
@@ -665,62 +609,63 @@
     wire.drain()
 
 
-def backward(
-    queries, pairs, squares, grad_context, seg_ids, gain, hidden, out_grad,
-    hidden_all, token_rows, q_weight, kv_weight, o_weight,
+def body(
+    source, row_token, seg_ids, stitch_weight, norm_gain, q_weight, kv_weight, o_weight, out_grad
 ):
     rows, columns = out_grad.shape
-    tokens, features = token_rows.shape
-    half = jnp.bfloat16
-    chunks = pltpu.VMEM((4, 2, rows, columns), half)
-    pair = pltpu.VMEM((rows, HD), half)
-    wide_shape = pltpu.VMEM((rows, q_weight.shape[1]), half)
+    source_rows, features = source.shape
+    tokens, width, heads = 16 * source_rows, 16 * columns, q_weight.shape[1]
+    kind = jnp.bfloat16
+
+    def on_chip(*shape, dtype=kind):
+        return pltpu.VMEM(shape, dtype)
+
     return pl.pallas_call(
-        backward_kernel,
+        step_kernel,
         out_shape=(
-            jax.ShapeDtypeStruct((rows, columns), half),
+            jax.ShapeDtypeStruct((rows, columns), kind),
             jax.ShapeDtypeStruct((features, columns), jnp.float32),
         ),
-        in_specs=[ON_CHIP] * 9 + [ANYWHERE] * 5,
+        in_specs=[ANYWHERE] + [ON_CHIP] * 3 + [ANYWHERE, ON_CHIP] + [ANYWHERE] * 4,
         out_specs=(ON_CHIP, ON_CHIP),
         scratch_shapes=[
-            pltpu.SemaphoreType.DMA((80,)),
-            pltpu.SemaphoreType.DMA((80,)),
-            pltpu.SemaphoreType.DMA((2,)),
+            pltpu.SemaphoreType.DMA((200,)),
+            pltpu.SemaphoreType.DMA((200,)),
+            pltpu.SemaphoreType.DMA((8,)),
             pltpu.SemaphoreType.DMA((5,)),
-            pltpu.VMEM(q_weight.shape, half),
-            pltpu.VMEM(kv_weight.shape, half),
-            pltpu.VMEM(o_weight.shape, half),
-            pltpu.VMEM(hidden_all.shape, half),
-            pltpu.VMEM(token_rows.shape, half),
-            pltpu.VMEM((tokens, columns), half),
-            pltpu.VMEM((rows, columns), half),
-            wide_shape, wide_shape, wide_shape, pair, pair, pair, pair, pair,
+            on_chip(*stitch_weight.shape),
+            on_chip(*q_weight.shape),
+            on_chip(*kv_weight.shape),
+            on_chip(*o_weight.shape),
+            on_chip(tokens, features),
+            on_chip(rows, width),
+            on_chip(rows, width),
+            on_chip(tokens, columns),
+            on_chip(tokens, features),
+            on_chip(rows, columns),
+            on_chip(rows, heads, dtype=jnp.float32),
+            on_chip(rows, HD, dtype=jnp.float32),
+            on_chip(rows, HD, dtype=jnp.float32),
+            on_chip(rows, heads),
+            on_chip(rows, HD, dtype=jnp.float32),
+            on_chip(rows, HD, dtype=jnp.float32),
+            on_chip(tokens, columns),
+            on_chip(rows, columns),
         ]
-        + [chunks] * 6
+        + [on_chip(rows, heads)] * 3
+        + [on_chip(rows, HD)] * 5
+        + [on_chip(4, 2, rows, columns)] * 2
+        + scatter_buffers(rows, columns, 128)
         + scatter_buffers(rows, columns, 128)
         + scatter_buffers(rows, columns, 64),
         compiler_params=pltpu.CompilerParams(
-            collective_id=2, has_side_effects=True, vmem_limit_bytes=60 << 20
+            collective_id=1, has_side_effects=True, vmem_limit_bytes=60 << 20
         ),
-        cost_estimate=pl.CostEstimate(flops=10 << 30, bytes_accessed=200 << 20, transcendentals=0),
-        name="backward",
+        cost_estimate=pl.CostEstimate(flops=30 << 30, bytes_accessed=200 << 20, transcendentals=0),
+        name="step",
     )(
-        queries, pairs, squares, grad_context, jnp.asarray(frequencies())[None], seg_ids,
-        gain.reshape(1, -1), hidden, out_grad, hidden_all, token_rows, q_weight, kv_weight,
-        o_weight,
-    )
-
-
-def body(
-    source, row_token, seg_ids, stitch_weight, norm_gain, q_weight, kv_weight, o_weight, out_grad
-):
-    token_rows, hidden_all, hidden, queries, pairs, squares, grad_context = forward(
-        source, row_token, stitch_weight, norm_gain, q_weight, kv_weight, o_weight, out_grad
-    )
-    return backward(
-        queries, pairs, squares, grad_context, seg_ids, norm_gain, hidden,
-        out_grad, hidden_all, token_rows, q_weight, kv_weight, o_weight,
+        source, row_token.reshape(1, -1), seg_ids, jnp.asarray(frequencies())[None], stitch_weight,
+        norm_gain.reshape(1, -1), q_weight, kv_weight, o_weight, out_grad,
     )
 
 

time: 160 us -> 153 us (0.956)
  Pallas kernels: 154 us -> 147 us
    pallas_call x2 -> x1, Pallas kernels: 154 us -> 147 us  [body(): pl.pallas_call(step_kernel, out_shape=(jax.ShapeDtypeStruct((rows, column...]
where the time goes in v4:
time: 153 us; the launch traced here: 152 us
  Pallas kernels  147 us (96%)
  local copies, waits for them, and re-layouts  4.75 us (3%)
    pallas_call x1, Pallas kernels, body(): pl.pallas_call(step_kernel, out_shape=(jax.ShapeDtypeStruct((rows, column...  147 us
    unnamed x2, local copies, waits for them, and re-layouts  4.75 us

profile of v4, /device:TPU:0, one launch (start us, length us, event | category | flops | bytes accessed | tf_op | source)
XLA Modules:
  0.0 152.2 jit_solution(14550588107934213440)
XLA Ops:
  0.6 146.8 %step.1 = (bf16[256,512]{1,0:T(8,128)(2,1)}, f32[1024,512]{1,0:T(8,128)}) custom-call(bf16[128,1024]{1,0:T(8,128)(2,1)} %source.1, s32[1,2048]{1,0:T(1,128)} %bitcast.3, s32[1,256]{1,0:T(1,128)} %seg_row.1, f32[1,128]{1,0:T(1,128)} %constant.4.rates, bf16[1024,512]{1,0:T(8,128)(2,1)} %stitch.1, f32[1,8192]{1,0:T(1,128)} %bitcast.2, bf16[8192,512]{1,0:T(8,128)(2,1)} %q_hbm.1, ...), custom_call_target="tpu_custom_call" | custom-call | flops 32212254720 | bytes 209715200 | tf_op jit(solution)/shard_map/step/pallas_call | solution.py:623
  147.5 1.7 %copy.14 = bf16[256,512]{1,0:T(8,128)(2,1)} copy(bf16[256,512]{1,0:T(8,128)(2,1)} %get-tuple-element.4) | data formatting | bytes 524288
  149.1 3.1 %copy.15 = f32[1024,512]{1,0:T(8,128)} copy(f32[1024,512]{1,0:T(8,128)} %get-tuple-element.5) | data formatting | bytes 4194304

commit v5 on v4

--- a/solution.py
+++ b/solution.py
@@ -383,11 +383,14 @@
             else:
                 token_part[there, :] = token_part[there, :] + moved
 
-    def place_late(tile):
-        total = wide(token_part[tile_of(tile), :])
-        for slot, (step, across) in enumerate(late):
-            total = total + dot(placed(tile, row_token[:, block_of(step, across)]), product[slot][...])
-        token_part[tile_of(tile), :] = total.astype(jnp.bfloat16)
+    def place_late(step):
+        tile = lax.rem(tok.ring + step, 4)
+        there = tile_of(tile, 2 * rows)
+        total = wide(token_part[there, :])
+        for slot, place in enumerate(late):
+            taken = row_token[:, block_of(*place)]
+            total = total + dot(placed(tile, taken, 2 * rows), product[slot][...])
+        token_part[there, :] = total.astype(jnp.bfloat16)
 
     def nothing(step, across):
         pass
@@ -397,8 +400,8 @@
         64, local.at[pl.ds(0, 2)], "source", source_ready,
     )
     gathering = gather_steps(
-        tp, wire, shard_views(out_grad, rows, 192), column_views(gradient_in, rows, columns, 192),
-        192, local.at[pl.ds(2, 2)], "gradient", nothing,
+        tp, wire, shard_views(out_grad, rows, 128), column_views(gradient_in, rows, columns, 128),
+        128, local.at[pl.ds(2, 2)], "gradient", nothing,
     )
     for _ in range(3):
         advance(fetching)
@@ -416,9 +419,10 @@
     def finish(half, value):
         hidden[part_of(half, rows, cut), :] = value.astype(hidden.dtype)
 
-    for step, across in ORDER:
-        place_late(tok.index(step, across))
-        scatter_first(tok, wire, part, buffers[0], buffers[1], cut, "hidden", step, across)
+    for step in (1, 3, 2, 0):
+        place_late(step)
+        for across in (1, 0):
+            scatter_first(tok, wire, part, buffers[0], buffers[1], cut, "hidden", step, across)
     scattering = scatter_steps(tok, wire, part, finish, going, buffers, "hidden")
 
     def reorder(first, last):
@@ -461,9 +465,9 @@
         128, local.at[pl.ds(4, 2)], "all", hidden_ready,
     )
     advance(collecting)
-    run(gathering)
     reorder(tiles // 2, tiles * 3 // 4)
     advance(collecting)
+    run(gathering)
     reorder(tiles * 3 // 4, tiles)
     advance(collecting)
     pulls[1].wait()
@@ -506,15 +510,15 @@
     keys = jnp.where(is_key, own_pair[...], other_pair[...])
     values = jnp.where(is_key, other_pair[...], own_pair[...])
     scale = 1.0 / math.sqrt(HD)
-    grad_keys = jnp.zeros((rows, HD), jnp.float32)
-    grad_values = jnp.zeros((rows, HD), jnp.float32)
+    grad_keys = jnp.zeros((HD, rows), jnp.float32)
+    grad_values = jnp.zeros((HD, rows), jnp.float32)
     along = jnp.zeros((rows, 1), jnp.float32)
     for head in range(heads):
         lanes = pl.ds(head * HD, HD)
         query, gradient = queries_in[:, lanes], grad_context[:, lanes]
         scores = jnp.where(allowed, dot(query, keys, BY_ROWS) * scale, -1e30)
         exponents = jnp.exp(scores - jnp.max(scores, axis=1, keepdims=True))
-        attention = exponents / jnp.sum(exponents, axis=1, keepdims=True)
+        attention = exponents * (1.0 / jnp.sum(exponents, axis=1, keepdims=True))
         attention_half = attention.astype(half)
         context[:, lanes] = dot(attention_half, values).astype(half)
         grad_probs = dot(gradient, values, BY_ROWS)
@@ -523,10 +527,34 @@
         grad_query = unrotate(dot(score_gradient, keys)).astype(half)
         grad_queries[:, lanes] = grad_query
         along = along + jnp.sum(wide(grad_query) * queries[:, lanes], axis=1, keepdims=True)
-        grad_keys = grad_keys + dot(score_gradient, query, BY_COLUMNS)
-        grad_values = grad_values + dot(attention_half, gradient, BY_COLUMNS)
+        grad_keys = grad_keys + dot(query, score_gradient, BY_COLUMNS)
+        grad_values = grad_values + dot(gradient, attention_half, BY_COLUMNS)
+    grad_keys, grad_values = grad_keys.T, grad_values.T
     leaving_pair[...] = jnp.where(is_key, grad_values, grad_keys).astype(half)
     wire.put(leaving_pair, back_pair, sibling, "back")
+    first, second = later[:6], later[6:]
+    cut_first, cut_second = 128, 64
+    mine, leaving = (chunks_in_rows(rows_in, rows, columns, side) for side in (0, 1))
+    mine_out, leaving_out = (
+        chunks_in_columns(gradient_in, rows, columns, side) for side in (0, 1)
+    )
+
+    def mine_first(step, across, half):
+        return mine(step, across, half, cut_first)
+
+    def mine_second(step, across, half):
+        return mine_out(step, across, half, cut_second)
+
+
+    def output_term(slot):
+        here = pl.ds(pl.multiple_of(slot * columns, columns), columns)
+        return dot(context[...], o_in[:, here]).astype(half)
+
+    output_meeting = core_steps(
+        tp, wire, output_term, mine_out, leaving_out, by_core_out, "output"
+    )
+    for _ in range(5):
+        advance(output_meeting)
     wire.got(back_pair, sibling, "back")
     summed = jnp.where(is_key, grad_keys, grad_values) + wide(back_pair[...])
     pair_gradient = jnp.where(is_key, unrotate(summed), summed).astype(half)
@@ -541,24 +569,6 @@
         value = value + dot(grad_pairs[...], kv_in[here, :], BY_ROWS)
         return (inv * (gain[:, here] * value) - wide(hidden_in[:, here]) * pulled).astype(half)
 
-    def output_term(slot):
-        here = pl.ds(pl.multiple_of(slot * columns, columns), columns)
-        return dot(context[...], o_in[:, here]).astype(half)
-
-    first, second = later[:6], later[6:]
-    cut_first, cut_second = 128, 64
-    mine, leaving = (chunks_in_rows(rows_in, rows, columns, side) for side in (0, 1))
-    mine_out, leaving_out = (
-        chunks_in_columns(gradient_in, rows, columns, side) for side in (0, 1)
-    )
-
-    def mine_first(step, across, half):
-        return mine(step, across, half, cut_first)
-
-    def mine_second(step, across, half):
-        return mine_out(step, across, half, cut_second)
-
-
     def gradient_total(where, value):
         here = part_of(where, rows, cut_first)
         grad_hidden[here, :] = (wide(grad_hidden[here, :]) + value).astype(half)
@@ -575,7 +585,7 @@
             tp, wire, mine_first, first[0], first[1], cut_first, "gradient", step, across
         )
         advance(meeting)
-    run(core_steps(tp, wire, output_term, mine_out, leaving_out, by_core_out, "output"))
+    run(output_meeting)
     scattering = scatter_steps(
         tp, wire, mine_first, gradient_total, first[4:], first[:4], "gradient"
     )

time: 153 us -> 151 us (0.987)
  Pallas kernels: 147 us -> 145 us
where the time goes in v5:
time: 151 us
  Pallas kernels  145 us (96%)
  local copies, waits for them, and re-layouts  4.75 us (3%)
    pallas_call x1, Pallas kernels, body(): pl.pallas_call(step_kernel, out_shape=(jax.ShapeDtypeStruct((rows, column...  145 us
    unnamed x2, local copies, waits for them, and re-layouts  4.75 us

profile of v5, /device:TPU:0, one launch (start us, length us, event | category | flops | bytes accessed | tf_op | source)
XLA Modules:
  0.0 150.8 jit_solution(12091328522923646480)
XLA Ops:
  0.6 145.4 %step.1 = (bf16[256,512]{1,0:T(8,128)(2,1)}, f32[1024,512]{1,0:T(8,128)}) custom-call(bf16[128,1024]{1,0:T(8,128)(2,1)} %source.1, s32[1,2048]{1,0:T(1,128)} %bitcast.3, s32[1,256]{1,0:T(1,128)} %seg_row.1, f32[1,128]{1,0:T(1,128)} %constant.4.rates, bf16[1024,512]{1,0:T(8,128)(2,1)} %stitch.1, f32[1,8192]{1,0:T(1,128)} %bitcast.2, bf16[8192,512]{1,0:T(8,128)(2,1)} %q_hbm.1, ...), custom_call_target="tpu_custom_call" | custom-call | flops 32212254720 | bytes 209715200 | tf_op jit(solution)/shard_map/step/pallas_call | solution.py:633
  146.1 1.7 %copy.14 = bf16[256,512]{1,0:T(8,128)(2,1)} copy(bf16[256,512]{1,0:T(8,128)(2,1)} %get-tuple-element.4) | data formatting | bytes 524288
  147.7 3.1 %copy.15 = f32[1024,512]{1,0:T(8,128)} copy(f32[1024,512]{1,0:T(8,128)} %get-tuple-element.5) | data formatting | bytes 4194304

commit v6 on v5

--- a/solution.py
+++ b/solution.py
@@ -201,7 +201,7 @@
     if step:
         wire.put(
             mine(step, across, 1),
-            by_ring.at[4 - step, across],
+            by_ring.at[3 - step, across],
             group.device(step, 0),
             (name, "ring", 4 - step, across),
         )
@@ -214,9 +214,9 @@
         wire.got(by_pair.at[step], group.device(0, 1), (name, "pair", step))
         total = wide(mine(step, 0, 0)[...]) + wide(by_pair[step])
         if step:
-            going[step] = total.astype(jnp.bfloat16)
+            going[step - 1] = total.astype(jnp.bfloat16)
             wire.put(
-                going.at[step], by_ring_last.at[4 - step], group.device(step, 0),
+                going.at[step - 1], by_ring_last.at[3 - step], group.device(step, 0),
                 (name, "last", 4 - step),
             )
         else:
@@ -224,8 +224,8 @@
     for across in (1, 0):
         total = wide(mine(0, across, 1)[...])
         for step in (1, 3, 2):
-            wire.got(by_ring.at[step, across], group.device(step, 0), (name, "ring", step, across))
-            total = total + wide(by_ring[step, across])
+            wire.got(by_ring.at[step - 1, across], group.device(step, 0), (name, "ring", step, across))
+            total = total + wide(by_ring[step - 1, across])
         if across:
             going_last[...] = total.astype(jnp.bfloat16)
             wire.put(going_last, by_pair_last, group.device(0, 1), (name, "last"))
@@ -233,8 +233,8 @@
     wire.got(by_pair_last, group.device(0, 1), (name, "last"))
     finish(1, total + wide(by_pair_last[...]))
     for step in (1, 3, 2):
-        wire.got(by_ring_last.at[step], group.device(step, 0), (name, "last", step))
-        first_total = first_total + wide(by_ring_last[step])
+        wire.got(by_ring_last.at[step - 1], group.device(step, 0), (name, "last", step))
+        first_total = first_total + wide(by_ring_last[step - 1])
     finish(0, first_total)
 
 
@@ -242,10 +242,10 @@
     first, second, kind = cut, rows - cut, jnp.bfloat16
     return [
         pltpu.VMEM((4, first, columns), kind),
-        pltpu.VMEM((4, 2, second, columns), kind),
-        pltpu.VMEM((4, first, columns), kind),
+        pltpu.VMEM((3, 2, second, columns), kind),
+        pltpu.VMEM((3, first, columns), kind),
         pltpu.VMEM((second, columns), kind),
-        pltpu.VMEM((4, first, columns), kind),
+        pltpu.VMEM((3, first, columns), kind),
         pltpu.VMEM((second, columns), kind),
     ]
 
@@ -314,11 +314,11 @@
 
 def step_kernel(
     source, row_token, seg_row, rates, stitch, gain, q_hbm, kv_hbm, o_hbm, out_grad,
-    layer_out, stitch_grad,
+    layer_out, stitch_out,
     send, recv, local, loads,
     stitch_in, q_in, kv_in, o_in, rows_in, hidden_in, gradient_in,
     token_part, token_rows, hidden, queries, pairs, squares, grad_context,
-    cosines, sines, every_grad, grad_hidden,
+    cosines, sines, every_grad, grad_hidden, stitch_grad,
     queries_in, context, grad_queries, grad_pairs, own_pair, other_pair, leaving_pair, back_pair,
     by_core, by_core_out,
     *buffers,
@@ -597,6 +597,8 @@
         value = dot(token_rows[here, :], every_grad[here, :], BY_COLUMNS)
         if (step, across) == (0, 0):
             stitch_grad[...] = value
+        elif (step, across) == (2, 1):
+            stitch_out[...] = (stitch_grad[...] + value).astype(half)
         else:
             stitch_grad[...] += value
 
@@ -630,11 +632,11 @@
     def on_chip(*shape, dtype=kind):
         return pltpu.VMEM(shape, dtype)
 
-    return pl.pallas_call(
+    layer_out, stitch_grad = pl.pallas_call(
         step_kernel,
         out_shape=(
             jax.ShapeDtypeStruct((rows, columns), kind),
-            jax.ShapeDtypeStruct((features, columns), jnp.float32),
+            jax.ShapeDtypeStruct((features, columns), kind),
         ),
         in_specs=[ANYWHERE] + [ON_CHIP] * 3 + [ANYWHERE, ON_CHIP] + [ANYWHERE] * 4,
         out_specs=(ON_CHIP, ON_CHIP),
@@ -661,6 +663,7 @@
             on_chip(rows, HD, dtype=jnp.float32),
             on_chip(tokens, columns),
             on_chip(rows, columns),
+            on_chip(features, columns, dtype=jnp.float32),
         ]
         + [on_chip(rows, heads)] * 3
         + [on_chip(rows, HD)] * 5
@@ -677,6 +680,7 @@
         source, row_token.reshape(1, -1), seg_ids, jnp.asarray(frequencies())[None], stitch_weight,
         norm_gain.reshape(1, -1), q_weight, kv_weight, o_weight, out_grad,
     )
+    return layer_out, stitch_grad.astype(jnp.float32)
 
 
 def solution(mesh):

time: 151 us -> 151 us (level)
  local copies, waits for them, and re-layouts: 4.75 us -> 1.67 us
  other arithmetic: 0 us -> 2.84 us
    unnamed x2 -> x1, local copies, waits for them, and re-layouts: 4.75 us -> 1.67 us
    convert_element_type x0 -> x1, other arithmetic: none -> 2.84 us  [body(): return (layer_out, stitch_grad.astype(jnp.float32))]
where the time goes in v6:
time: 151 us; the launch traced here: 150 us
  Pallas kernels  145 us (96%)
  other arithmetic  2.84 us (2%)
  local copies, waits for them, and re-layouts  1.67 us (1%)
    pallas_call x1, Pallas kernels, body(): pl.pallas_call(step_kernel, out_shape=(jax.ShapeDtypeStruct((rows, column...  145 us

profile of v6, /device:TPU:0, one launch (start us, length us, event | category | flops | bytes accessed | tf_op | source)
XLA Modules:
  0.0 150.2 jit_solution(10902747583745360346)
XLA Ops:
  0.6 145.1 %step.1 = (bf16[256,512]{1,0:T(8,128)(2,1)}, bf16[1024,512]{1,0:T(8,128)(2,1)}) custom-call(bf16[128,1024]{1,0:T(8,128)(2,1)} %source.1, s32[1,2048]{1,0:T(1,128)} %bitcast.3, s32[1,256]{1,0:T(1,128)} %seg_row.1, f32[1,128]{1,0:T(1,128)} %constant.4.rates, bf16[1024,512]{1,0:T(8,128)(2,1)} %stitch.1, f32[1,8192]{1,0:T(1,128)} %bitcast.2, ...), custom_call_target="tpu_custom_call" | custom-call | flops 32212254720 | bytes 209715200 | tf_op jit(solution)/shard_map/step/pallas_call | solution.py:635
  145.7 2.8 %convert_element_type.3 = f32[1024,512]{1,0:T(8,128)} convert(bf16[1024,512]{1,0:T(8,128)(2,1)} %get-tuple-element.5) | non-fusion elementwise | flops 524288 | bytes 3145728 | tf_op jit(solution)/shard_map/convert_element_type | solution.py:683
  148.6 1.7 %copy.13 = bf16[256,512]{1,0:T(8,128)(2,1)} copy(bf16[256,512]{1,0:T(8,128)(2,1)} %get-tuple-element.8) | data formatting | bytes 524288

commit v7 on v6

--- a/solution.py
+++ b/solution.py
@@ -590,6 +590,8 @@
         tp, wire, mine_first, gradient_total, first[4:], first[:4], "gradient"
     )
     advance(scattering)
+    for step, across in ORDER:
+        scatter_first(tp, wire, mine_second, second[0], second[1], cut_second, "output", step, across)
     run(scattering)
 
     def pack_ready(step, across):
@@ -608,8 +610,6 @@
         cut_grad, local.at[pl.ds(6, 2)], "every", pack_ready,
     )
     advance(gathering)
-    for step, across in ORDER:
-        scatter_first(tp, wire, mine_second, second[0], second[1], cut_second, "output", step, across)
     scattering = scatter_steps(
         tp, wire, mine_second, output_total, second[4:], second[:4], "output"
     )

time: 151 us -> 150 us (level)
  no operation moved by 1% of the time
where the time goes in v7:
time: 150 us
  Pallas kernels  145 us (97%)
  other arithmetic  2.84 us (2%)
  local copies, waits for them, and re-layouts  1.67 us (1%)
    pallas_call x1, Pallas kernels, body(): pl.pallas_call(step_kernel, out_shape=(jax.ShapeDtypeStruct((rows, column...  145 us

profile of v7, /device:TPU:0, one launch (start us, length us, event | category | flops | bytes accessed | tf_op | source)
XLA Modules:
  0.0 150.2 jit_solution(7204788806052710644)
XLA Ops:
  0.6 145.0 %step.1 = (bf16[256,512]{1,0:T(8,128)(2,1)}, bf16[1024,512]{1,0:T(8,128)(2,1)}) custom-call(bf16[128,1024]{1,0:T(8,128)(2,1)} %source.1, s32[1,2048]{1,0:T(1,128)} %bitcast.3, s32[1,256]{1,0:T(1,128)} %seg_row.1, f32[1,128]{1,0:T(1,128)} %constant.4.rates, bf16[1024,512]{1,0:T(8,128)(2,1)} %stitch.1, f32[1,8192]{1,0:T(1,128)} %bitcast.2, ...), custom_call_target="tpu_custom_call" | custom-call | flops 32212254720 | bytes 209715200 | tf_op jit(solution)/shard_map/step/pallas_call | solution.py:635
  145.7 2.8 %convert_element_type.3 = f32[1024,512]{1,0:T(8,128)} convert(bf16[1024,512]{1,0:T(8,128)(2,1)} %get-tuple-element.5) | non-fusion elementwise | flops 524288 | bytes 3145728 | tf_op jit(solution)/shard_map/convert_element_type | solution.py:683
  148.5 1.7 %copy.13 = bf16[256,512]{1,0:T(8,128)(2,1)} copy(bf16[256,512]{1,0:T(8,128)(2,1)} %get-tuple-element.8) | data formatting | bytes 524288
